TPU v7x, 32 devices: a whole 2x2x4 slice. The times are simulated.
32 devices in a mesh: dp: 8 (over z, y), tensor: 4 (over x, core).
Axes of the slice: x: 2, y: 2, z: 4, core: 2. Of those that a mesh axis runs over, the one named last changes fastest.
Arguments:
- tokens: bfloat16 [3, 4096, 1536], P(None, ('dp', 'tensor')), may hold values from -6 to 6
- lengths: int32 [3, 32, 6], P(None, ('dp', 'tensor')), may hold values from 1 to 64, 128 in all within a row
- first_gain: bfloat16 [1536], P(('dp', 'tensor')), may hold values from 0.099609375 to 1.8984375
- query_weight: bfloat16 [1536, 1536], P(('dp', 'tensor')), may hold values from -0.15625 to 0.15625
- key_weight: bfloat16 [1536, 768], P(('dp', 'tensor')), may hold values from -0.15625 to 0.15625
- value_weight: bfloat16 [1536, 768], P(('dp', 'tensor')), may hold values from -0.15625 to 0.15625
- output_weight: bfloat16 [1536, 1536], P(('dp', 'tensor')), may hold values from -0.4375 to 0.4375
- second_gain: bfloat16 [1536], P(('dp', 'tensor')), may hold values from 0.099609375 to 1.8984375
- gate_weight: bfloat16 [1536, 4096], P('dp', 'tensor'), may hold values from -0.15625 to 0.15625
- up_weight: bfloat16 [1536, 4096], P('dp', 'tensor'), may hold values from -0.15625 to 0.15625
- down_weight: bfloat16 [4096, 1536], P('tensor', 'dp'), may hold values from -0.09375 to 0.09375
- cotangent: bfloat16 [3, 4096, 1536], P(None, ('dp', 'tensor')), may hold values from -6 to 6
Outputs:
- layer_out: bfloat16 [3, 4096, 1536], P(None, ('dp', 'tensor'))
- input_grad: float32 [3, 4096, 1536], P(None, ('dp', 'tensor'))
- first_gain_grad: float32 [1536], P(('dp', 'tensor'))
- query_grad: float32 [1536, 1536], P(('dp', 'tensor'))
- key_grad: float32 [1536, 768], P(('dp', 'tensor'))
- value_grad: float32 [1536, 768], P(('dp', 'tensor'))
- output_grad: float32 [1536, 1536], P(('dp', 'tensor'))
- second_gain_grad: float32 [1536], P(('dp', 'tensor'))
- gate_grad: float32 [1536, 4096], P('dp', 'tensor')
- up_grad: float32 [1536, 4096], P('dp', 'tensor')
- down_grad: float32 [4096, 1536], P('tensor', 'dp')
Inputs may be any that keep to these rules, and one draw needn't show every extreme that they name: Row lengths[m, p] splits the 128 rows of pack p of micro-batch m into 6 runs in order, summing to 128; the first 5 runs are sequences, the last is padding; no run is longer than 64 rows.
All inputs are finite; a program needn't handle non-finite values.
Results may differ from a plain program's by a relative error of at most 0.013.
Values may be sent and summed in bfloat16 or wider, within the bound.
No kernel may reach another device: no remote copies, remote signals or barrier semaphores. Data moves between devices by JAX's collectives and lax.ppermute only.
A program may use at most 192 MiB of HBM per device.

v0:
```python
import math
import jax
import jax.numpy as jnp
from jax import lax
from jax.sharding import PartitionSpec as P

HEADS = 16
KV_HEADS = 8
HEAD = 96
SLOTS = 6
GROUP = HEADS // KV_HEADS
LANES = 128
EPSILON = 1e-05
ROPE_BASE = 100000.0
NEG_LARGE = -1e30
AXES = ("dp", "tensor")
bf16 = jnp.bfloat16
f32 = jnp.float32


def pack_layout(seq_lengths, row_count):
    seq_ends = jnp.cumsum(seq_lengths)
    seq_starts = seq_ends - seq_lengths
    row_index = jnp.arange(row_count, dtype=jnp.int32)
    segment = jnp.sum((row_index[:, None] >= seq_ends[None, :]).astype(jnp.int32), axis=1)
    owner_hot = segment[:, None] == jnp.arange(seq_lengths.shape[0], dtype=jnp.int32)[None, :]
    position = row_index - jnp.sum(jnp.where(owner_hot, seq_starts[None, :], 0), axis=1)
    return (segment, position)


def rotary_tables(position, head_size):
    half_size = head_size // 2
    freq_index = jnp.arange(half_size, dtype=f32)
    inverse = jnp.exp(freq_index * (-2.0 / head_size) * math.log(ROPE_BASE))
    angles = position.astype(f32)[..., None] * inverse
    return (jnp.cos(angles), jnp.sin(angles))


def rotate(vectors, cosine, sine_part):
    half_size = vectors.shape[-1] // 2
    lower_half = vectors[..., :half_size]
    upper_half = vectors[..., half_size:]
    cosine = cosine[..., None, :]
    sine_part = sine_part[..., None, :]
    return jnp.concatenate(
        [
            lower_half * cosine - upper_half * sine_part,
            upper_half * cosine + lower_half * sine_part,
        ],
        axis=-1,
    )


def product(left_side, right_side):
    return jnp.dot(left_side, right_side, preferred_element_type=f32)


def across(left_side, right_side):
    return lax.dot_general(
        left_side, right_side, (((0,), (0,)), ((), ())), preferred_element_type=f32
    )


def against(left_side, right_side):
    return lax.dot_general(
        left_side, right_side, (((1,), (1,)), ((), ())), preferred_element_type=f32
    )


def bits_of(size):
    return [1 << k for k in range(size.bit_length() - 1)]


def near_first(size):
    masks = bits_of(size)
    return masks[:1] + masks[:0:-1]


def far_first(size):
    return bits_of(size)[::-1]


def rel_source(me, masks, block, count):
    place = jnp.arange(count, dtype=jnp.int32)
    step = place // block
    delta = jnp.zeros_like(step)
    for k, mask in enumerate(masks):
        delta = delta + (step >> k & 1) * mask
    return (me ^ delta) * block + place % block


def one_hot(source):
    count = source.shape[0]
    rows = lax.broadcasted_iota(jnp.int32, (count, count), 0)
    return (rows == source[None, :]).astype(bf16)


def join(parts):
    return parts[0] if len(parts) == 1 else jnp.concatenate(parts, axis=0)


def program(sizes):
    dp_n, tp_n = (sizes["dp"], sizes["tensor"])
    world = dp_n * tp_n

    def swap(array, mask):
        return lax.ppermute(array, AXES, [(i, i ^ mask) for i in range(world)])

    def gather(own, masks, loose):
        held = [own]
        for k, mask in enumerate(masks):
            got = [swap(part, mask) for part in held]
            held = held + got
            if k < len(masks) - loose:
                held = [join(held)]
        return held

    def per_device(
        tokens,
        lengths,
        first_gain,
        query_weight,
        key_weight,
        value_weight,
        output_weight,
        second_gain,
        gate_weight,
        up_weight,
        down_weight,
        cotangent,
    ):
        micro, per_pack, width = tokens.shape
        rows = micro * per_pack
        qw, kw = (query_weight.shape[1], key_weight.shape[1])
        ff = gate_weight.shape[1]
        wide = qw + 2 * kw
        shard = query_weight.shape[0]
        dp_i, t_i = (lax.axis_index("dp"), lax.axis_index("tensor"))
        me = dp_i * tp_n + t_i
        dp_attn = [m * tp_n for m in near_first(dp_n)]
        t_bits = bits_of(tp_n)[::-1]
        attn_masks = dp_attn + t_bits
        mlp_masks = [m * tp_n for m in far_first(dp_n)]
        x_low = tokens.reshape(rows, width)
        dy_low = cotangent.reshape(rows, width)
        gains = jnp.pad(jnp.stack([first_gain, second_gain], axis=1), ((0, 0), (0, LANES - 2)))
        own_qkv = jnp.concatenate([query_weight, key_weight, value_weight, gains], axis=1)
        own_gu = jnp.concatenate([gate_weight, up_weight], axis=1)
        own_down = down_weight.T

        def gather_attn(own):
            held = gather(own, dp_attn, 2)
            far = [swap(part, t_bits[0]) for part in held]
            pieces = [join(held), join(far)]
            for mask in t_bits[1:]:
                pieces = pieces + [swap(part, mask) for part in pieces]
            return pieces

        qkv_pieces = gather_attn(own_qkv)
        out_pieces = gather_attn(output_weight)
        gu_full = join(gather(own_gu, mlp_masks, 3))
        down_full = join(gather(own_down, mlp_masks, 3))
        n_pieces = len(qkv_pieces)
        part = width // n_pieces
        pick_attn = one_hot(rel_source(me, attn_masks, shard, width))
        mlp_source = rel_source(dp_i, [m // tp_n for m in mlp_masks], shard * tp_n, width)
        pick_mlp = one_hot(mlp_source)

        def order(array, pick):
            return product(array, pick).astype(bf16)

        def restore(array, pick):
            return against(array, pick)

        gains_rel = jnp.concatenate([piece[:, wide : wide + 2] for piece in qkv_pieces], axis=0)
        g1_rel = gains_rel[:, 0].astype(f32)
        g2 = restore(gains_rel[:, 1][None, :], pick_attn)[0]
        segment, position = jax.vmap(lambda own: pack_layout(own, per_pack))(lengths[:, 0])
        cosine, sine_part = rotary_tables(position, HEAD)
        row_index = jnp.arange(per_pack, dtype=jnp.int32)
        allowed = (
            (segment[:, :, None] == segment[:, None, :])
            & (row_index[None, None, :] <= row_index[None, :, None])
            & (segment < SLOTS - 1)[:, :, None]
        )[:, None, None]
        factor = 1.0 / math.sqrt(HEAD)
        inputs = x_low.astype(f32)
        r1 = lax.rsqrt(jnp.mean(inputs * inputs, axis=1, keepdims=True) + EPSILON)
        x_rel = order(x_low, pick_attn).astype(f32)
        n1_rel = (x_rel * r1 * g1_rel).astype(bf16)
        n1_parts = [n1_rel[:, k * part : (k + 1) * part] for k in range(n_pieces)]
        qkv = sum((product(a, b) for a, b in zip(n1_parts, qkv_pieces)))
        shape = (micro, per_pack)
        queries = rotate(qkv[:, :qw].reshape(shape + (HEADS, HEAD)), cosine, sine_part)
        queries = queries.astype(bf16).reshape(shape + (KV_HEADS, GROUP, HEAD))
        keys = rotate(
            qkv[:, qw : qw + kw].reshape(shape + (KV_HEADS, HEAD)), cosine, sine_part
        ).astype(bf16)
        values = qkv[:, qw + kw : wide].astype(bf16).reshape(shape + (KV_HEADS, HEAD))
        scores = jnp.einsum("pqhgd,pkhd->phgqk", queries, keys, preferred_element_type=f32) * factor
        row_peak = jnp.max(jnp.where(allowed, scores, NEG_LARGE), axis=-1, keepdims=True)
        raised = jnp.where(allowed, jnp.exp(jnp.where(allowed, scores - row_peak, 0.0)), 0.0)
        totals = jnp.sum(raised, axis=-1, keepdims=True)
        probs = raised / jnp.where(totals > 0, totals, 1.0)
        probs_low = probs.astype(bf16)
        attended = jnp.einsum("phgqk,pkhd->pqhgd", probs_low, values, preferred_element_type=f32)
        attended = attended.reshape(rows, qw).astype(bf16)
        att_rel = order(attended, pick_attn)
        att_parts = [att_rel[:, k * part : (k + 1) * part] for k in range(n_pieces)]
        middle = inputs + sum((product(a, b) for a, b in zip(att_parts, out_pieces)))
        r2 = lax.rsqrt(jnp.mean(middle * middle, axis=1, keepdims=True) + EPSILON)
        n2 = (middle * r2 * g2).astype(bf16)
        n2_rel = order(n2, pick_mlp)
        dy_rel = order(dy_low, pick_mlp)

        def spread(own):
            return join(gather(own, t_bits, tp_n))

        def collect(partial):
            for mask in t_bits[::-1]:
                half = partial.shape[0] // 2
                got = swap(partial[half:].astype(bf16), mask)
                partial = partial[:half].astype(f32) + got.astype(f32)
            return partial

        dy_all = spread(dy_rel)
        n2_all = spread(n2_rel)
        gu = product(n2_all, gu_full)
        gate, up = (gu[:, :ff], gu[:, ff:])
        sig = jax.nn.sigmoid(gate)
        hidden = (gate * sig * up).astype(bf16)
        dhid = product(dy_all, down_full)
        dgate = (dhid * up * sig * (1.0 + gate * (1.0 - sig))).astype(bf16)
        dup = (dhid * gate * sig).astype(bf16)
        dgu = jnp.concatenate([dgate, dup], axis=1)
        dn2 = restore(collect(against(dgu, gu_full).astype(bf16)).astype(bf16), pick_mlp)
        down_sum = collect(against(hidden, down_full).astype(bf16)).astype(bf16)
        layer_out = (middle + restore(down_sum, pick_mlp)).astype(bf16)

        def reduce_rows(own_half, sent_half, masks):
            total = own_half() + swap(sent_half().astype(bf16), masks[0]).astype(f32)
            for mask in masks[1:]:
                half = total.shape[0] // 2
                got = swap(total[half:].astype(bf16), mask)
                total = total[:half] + got.astype(f32)
            return total

        half = width // 2

        def mlp_grad(left, right):
            return reduce_rows(
                lambda: across(left[:, :half], right),
                lambda: across(left[:, half:], right),
                mlp_masks[::-1],
            )

        down_grad = mlp_grad(dy_all, hidden).T
        gate_grad = mlp_grad(n2_all, dgate)
        up_grad = mlp_grad(n2_all, dup)
        dy = dy_low.astype(f32)
        weighted = dn2 * g2
        dmid = (
            dy
            + r2 * weighted
            - middle * (r2 * r2 * r2) * jnp.mean(weighted * middle, axis=1, keepdims=True)
        )
        dmb = dmid.astype(bf16)

        def attn_grad(lefts, right):
            held = [across(left, right) for left in lefts]
            for mask in t_bits[1:][::-1]:
                n = len(held) // 2
                got = [swap(piece.astype(bf16), mask) for piece in held[n:]]
                held = [a + b.astype(f32) for a, b in zip(held[:n], got)]
            return reduce_rows(lambda: held[0], lambda: held[1], [t_bits[0]] + dp_attn[::-1])

        output_grad = attn_grad(att_parts, dmb)
        datt_rel = jnp.concatenate([against(dmb, piece) for piece in out_pieces], axis=1)
        datt = restore(datt_rel.astype(bf16), pick_attn).astype(bf16)
        datt = datt.reshape(shape + (KV_HEADS, GROUP, HEAD))
        dprob = jnp.einsum("pqhgd,pkhd->phgqk", datt, values, preferred_element_type=f32)
        delta = jnp.sum(probs * dprob, axis=-1, keepdims=True)
        dscore = (probs * (dprob - delta)).astype(bf16)
        dvalue = jnp.einsum("phgqk,pqhgd->pkhd", probs_low, datt, preferred_element_type=f32)
        dqr = jnp.einsum("phgqk,pkhd->pqhgd", dscore, keys, preferred_element_type=f32) * factor
        dkr = jnp.einsum("phgqk,pqhgd->pkhd", dscore, queries, preferred_element_type=f32) * factor
        dq = rotate(dqr.reshape(shape + (HEADS, HEAD)), cosine, -sine_part)
        dk = rotate(dkr, cosine, -sine_part)
        dqkv = jnp.concatenate(
            [
                dq.astype(bf16).reshape(rows, qw),
                dk.astype(bf16).reshape(rows, kw),
                dvalue.astype(bf16).reshape(rows, kw),
            ],
            axis=1,
        )
        qkv_grad = attn_grad(n1_parts, dqkv)
        dn1_rel = jnp.concatenate([against(dqkv, piece[:, :wide]) for piece in qkv_pieces], axis=1)
        weighted = dn1_rel * g1_rel
        part_rel = r1 * weighted - x_rel * (r1 * r1 * r1) * jnp.mean(
            weighted * x_rel, axis=1, keepdims=True
        )
        high = part_rel.astype(bf16)
        low = (part_rel - high.astype(f32)).astype(bf16)
        input_grad = dmid + restore(high, pick_attn) + restore(low, pick_attn)
        own_wide = own_qkv[:, :wide].astype(f32)
        first_gain_grad = jnp.sum(own_wide * qkv_grad, axis=1) / first_gain.astype(f32)
        second = jnp.sum(
            gate_weight.astype(f32) * gate_grad + up_weight.astype(f32) * up_grad, axis=1
        )
        second = lax.psum(second, "tensor")
        second = lax.dynamic_slice(second, (t_i * shard,), (shard,))
        second_gain_grad = second / second_gain.astype(f32)
        return (
            layer_out.reshape(tokens.shape),
            input_grad.reshape(tokens.shape),
            first_gain_grad,
            qkv_grad[:, :qw],
            qkv_grad[:, qw : qw + kw],
            qkv_grad[:, qw + kw :],
            output_grad,
            second_gain_grad,
            gate_grad,
            up_grad,
            down_grad,
        )

    return per_device


def solution(mesh):
    rows = P(None, AXES, None)
    split = P(AXES, None)
    placed = (
        rows,
        rows,
        P(AXES),
        split,
        split,
        split,
        split,
        P(AXES),
        P("dp", "tensor"),
        P("dp", "tensor"),
        P("tensor", "dp"),
        rows,
    )
    return jax.shard_map(
        program(dict(mesh.shape)),
        mesh=mesh,
        in_specs=placed,
        out_specs=(
            rows,
            rows,
            P(AXES),
            split,
            split,
            split,
            split,
            P(AXES),
            P("dp", "tensor"),
            P("dp", "tensor"),
            P("tensor", "dp"),
        ),
        check_vma=False,
    )
```

profile of v0, /device:TPU:0, one launch (start us, length us, event | category | flops | bytes accessed | tf_op | source)
XLA Modules:
  0.0 805.7 jit_solution(15397457779507763800)
XLA Ops:
  0.7 4.1 collective-permute-start.30
  29.8 8.6 %collective-permute-done.4 = bf16[96,3200]{1,0:T(8,128)(2,1)S(1)} collective-permute-done((bf16[96,3200]{1,0:T(8,128)(2,1)S(1)}, bf16[96,3200]{1,0:T(8,128)(2,1)S(1)}, u32[]{:S(2)}, u32[]{:S(2)}) %collective-permute-start.4) | collective-permute-done | bytes 614432 | tf_op jit(solution)/shard_map/ppermute | solution.py:107
  39.7 27.5 %collective-permute-done.1 = bf16[96,3200]{1,0:T(8,128)(2,1)S(1)} collective-permute-done((bf16[96,3200]{1,0:T(8,128)(2,1)S(1)}, bf16[96,3200]{1,0:T(8,128)(2,1)S(1)}, u32[]{:S(2)}, u32[]{:S(2)}) %collective-permute-start.1) | collective-permute-done | bytes 614432 | tf_op jit(solution)/shard_map/ppermute | solution.py:107
  68.1 4.7 collective-permute-done.2
  76.1 8.4 %collective-permute-done.3 = bf16[96,3200]{1,0:T(8,128)(2,1)S(1)} collective-permute-done((bf16[96,3200]{1,0:T(8,128)(2,1)S(1)}, bf16[96,3200]{1,0:T(8,128)(2,1)S(1)}, u32[]{:S(2)}, u32[]{:S(2)}) %collective-permute-start.3) | collective-permute-done | bytes 614432 | tf_op jit(solution)/shard_map/ppermute | solution.py:107
  88.3 13.0 %collective-permute-done.6 = bf16[96,3200]{1,0:T(8,128)(2,1)S(1)} collective-permute-done((bf16[96,3200]{1,0:T(8,128)(2,1)S(1)}, bf16[96,3200]{1,0:T(8,128)(2,1)S(1)}, u32[]{:S(2)}, u32[]{:S(2)}) %collective-permute-start.6) | collective-permute-done | bytes 614432 | tf_op jit(solution)/shard_map/ppermute | solution.py:107
  102.2 9.9 %collective-permute-done.7 = bf16[96,3200]{1,0:T(8,128)(2,1)S(1)} collective-permute-done((bf16[96,3200]{1,0:T(8,128)(2,1)S(1)}, bf16[96,3200]{1,0:T(8,128)(2,1)S(1)}, u32[]{:S(2)}, u32[]{:S(2)}) %collective-permute-start.7) | collective-permute-done | bytes 614432 | tf_op jit(solution)/shard_map/ppermute | solution.py:107
  119.2 5.5 collective-permute-done.14
  126.7 4.3 collective-permute-done.15
  132.5 3.8 collective-permute-done.16
  141.3 7.3 collective-permute-done.34
  149.2 23.1 %collective-permute-done.23 = bf16[192,2048]{1,0:T(8,128)(2,1)S(1)} collective-permute-done((bf16[192,2048]{1,0:T(8,128)(2,1)}, bf16[192,2048]{1,0:T(8,128)(2,1)S(1)}, u32[]{:S(2)}, u32[]{:S(2)}) %collective-permute-start.23) | collective-permute-done | bytes 786464 | tf_op jit(solution)/shard_map/ppermute | solution.py:107
  180.7 4.3 multiply_convert_fusion.4
  185.1 3.6 fusion.149
  188.7 3.7 fusion.137
  211.0 3.7 subtract_convert_fusion.1
  254.1 18.8 %collective-permute-done.36 = bf16[192,1024]{1,0:T(8,128)(2,1)S(1)} collective-permute-done((bf16[192,1024]{1,0:T(8,128)(2,1)S(1)}, bf16[192,1024]{1,0:T(8,128)(2,1)S(1)}, u32[]{:S(2)}, u32[]{:S(2)}) %collective-permute-start.36) | collective-permute-done | bytes 393248 | tf_op jit(solution)/shard_map/ppermute | solution.py:107
  280.2 13.4 %collective-permute-done.28 = bf16[192,2048]{1,0:T(8,128)(2,1)S(1)} collective-permute-done((bf16[192,2048]{1,0:T(8,128)(2,1)}, bf16[192,2048]{1,0:T(8,128)(2,1)S(1)}, u32[]{:S(2)}, u32[]{:S(2)}) %collective-permute-start.28) | collective-permute-done | bytes 786464 | tf_op jit(solution)/shard_map/ppermute | solution.py:107
  295.1 13.2 %collective-permute-done.29 = bf16[192,2048]{1,0:T(8,128)(2,1)S(1)} collective-permute-done((bf16[192,2048]{1,0:T(8,128)(2,1)S(1)}, bf16[192,2048]{1,0:T(8,128)(2,1)S(1)}, u32[]{:S(2)}, u32[]{:S(2)}) %collective-permute-start.29) | collective-permute-done | bytes 786464 | tf_op jit(solution)/shard_map/ppermute | solution.py:107
  314.0 16.8 %fusion.176 = f32[1536,2048]{1,0:T(8,128)} fusion(bf16[1536,2048]{1,0:T(8,128)(2,1)S(1)} %copy-done.68, bf16[384,1536]{1,0:T(8,128)(2,1)S(1)} %collective-permute-done.22, bf16[384,1536]{1,0:T(8,128)(2,1)S(1)} %collective-permute-done.21, bf16[384,1536]{1,0:T(8,128)(2,1)S(1)} %collective-permute-done.20, bf16[384,1536]{1,0:T(8,128)(2,1)S(1)} %fusion.47), kind=kOutput, calls=%fused_computation.319 | convolution fusion | flops 9682550784 | bytes 23592960 | tf_op jit(solution)/shard_map/dot_general | solution.py:55
  330.8 15.0 %multiply_convert_fusion.1 = (bf16[1536,1024]{1,0:T(8,128)(2,1)S(1)}, bf16[1536,1024]{1,0:T(8,128)(2,1)}, bf16[1536,1024]{1,0:T(8,128)(2,1)}) fusion(f32[1536,2048]{1,0:T(8,128)} %fusion.176, bf16[1536,1024]{1,0:T(8,128)(2,1)} %constant_dynamic-update-slice_fusion.31, bf16[384,1536]{1,0:T(8,128)(2,1)} %copy-done.42, bf16[384,1536]{1,0:T(8,128)(2,1)} %copy-done.41, ...), kind=kOutput, calls=%fused_computation.19 | convolution fusion | flops 4875878400 | bytes 29884416 | tf_op jit(solution)/shard_map/dot_general | solution.py:55
  345.8 6.8 fusion.92
  354.5 3.8 fusion.89
  359.8 15.1 %convolution_convert_fusion.1 = bf16[1536,1536]{1,0:T(8,128)(2,1)} fusion(bf16[1536,2048]{1,0:T(8,128)(2,1)} %constant_dynamic-update-slice_fusion.22, bf16[1536,1024]{1,0:T(8,128)(2,1)} %get-tuple-element.19, bf16[1536,1024]{1,0:T(8,128)(2,1)S(1)} %get-tuple-element.18), kind=kOutput, calls=%fused_computation.14 | convolution fusion | flops 9678618624 | bytes 17301504 | tf_op jit(solution)/shard_map/dot_general | solution.py:65
  374.9 3.8 fusion.86
  379.3 7.4 convolution_convert_fusion
  390.3 4.1 convert_add_fusion.3
  396.0 28.0 %collective-permute-done.59 = bf16[768,1024]{1,0:T(8,128)(2,1)} collective-permute-done((bf16[768,1024]{1,0:T(8,128)(2,1)}, bf16[768,1024]{1,0:T(8,128)(2,1)}, u32[]{:S(2)}, u32[]{:S(2)}) %collective-permute-start.59) | collective-permute-done | bytes 1572896 | tf_op jit(solution)/shard_map/ppermute | solution.py:107
  424.0 4.1 convert_add_fusion.4
  429.7 24.8 %collective-permute-done.56 = bf16[768,1024]{1,0:T(8,128)(2,1)S(1)} collective-permute-done((bf16[768,1024]{1,0:T(8,128)(2,1)}, bf16[768,1024]{1,0:T(8,128)(2,1)S(1)}, u32[]{:S(2)}, u32[]{:S(2)}) %collective-permute-start.56) | collective-permute-done | bytes 1572896 | tf_op jit(solution)/shard_map/ppermute | solution.py:107
  463.5 22.9 %collective-permute-done.57 = bf16[384,1024]{1,0:T(8,128)(2,1)S(1)} collective-permute-done((bf16[384,1024]{1,0:T(8,128)(2,1)S(1)}, bf16[384,1024]{1,0:T(8,128)(2,1)S(1)}, u32[]{:S(2)}, u32[]{:S(2)}) %collective-permute-start.57) | collective-permute-done | bytes 786464 | tf_op jit(solution)/shard_map/ppermute | solution.py:107
  496.8 9.9 %collective-permute-done.61 = bf16[192,1024]{1,0:T(8,128)(2,1)S(1)} collective-permute-done((bf16[192,1024]{1,0:T(8,128)(2,1)S(1)}, bf16[192,1024]{1,0:T(8,128)(2,1)S(1)}, u32[]{:S(2)}, u32[]{:S(2)}) %collective-permute-start.61) | collective-permute-done | bytes 393248 | tf_op jit(solution)/shard_map/ppermute | solution.py:107
  506.6 4.2 collective-permute-done.58
  512.9 29.6 %psum.7 = f32[192]{0:T(256)} all-reduce(f32[192]{0:T(256)} %get-tuple-element.11), channel_id=1, replica_groups=mesh['dp'=8,'tensor'=4] {'tensor'}, use_global_device_ids=true, to_apply=%region_12.13 | all-reduce | flops 192 | bytes 1536 | tf_op jit(solution)/shard_map/psum | solution.py:311
  546.0 4.5 multiply_reduce_fusion.1
  566.9 6.2 reshape.247
  573.1 5.2 copy.140
  578.3 3.8 fusion.102
  609.5 3.7 subtract_convert_fusion
  615.2 4.1 convert_element_type.310
  645.4 4.4 fusion.5
  649.9 69.7 %collective-permute-done.52 = bf16[384,1536]{1,0:T(8,128)(2,1)S(1)} collective-permute-done((bf16[384,1536]{1,0:T(8,128)(2,1)S(1)}, bf16[384,1536]{1,0:T(8,128)(2,1)S(1)}, u32[]{:S(2)}, u32[]{:S(2)}) %collective-permute-start.52) | collective-permute-done | bytes 1179680 | tf_op jit(solution)/shard_map/ppermute | solution.py:107
  724.5 6.1 fusion.40
  730.6 5.8 collective-permute-done.53
  739.2 27.2 %collective-permute-done.47 = bf16[192,3072]{1,0:T(8,128)(2,1)S(1)} collective-permute-done((bf16[192,3072]{1,0:T(8,128)(2,1)S(1)}, bf16[192,3072]{1,0:T(8,128)(2,1)S(1)}, u32[]{:S(2)}, u32[]{:S(2)}) %collective-permute-start.47) | collective-permute-done | bytes 1179680 | tf_op jit(solution)/shard_map/ppermute | solution.py:107
  767.3 4.6 fusion.49
  773.4 20.7 %collective-permute-done.48 = bf16[96,3072]{1,0:T(8,128)(2,1)S(1)} collective-permute-done((bf16[96,3072]{1,0:T(8,128)(2,1)S(1)}, bf16[96,3072]{1,0:T(8,128)(2,1)S(1)}, u32[]{:S(2)}, u32[]{:S(2)}) %collective-permute-start.48) | collective-permute-done | bytes 589856 | tf_op jit(solution)/shard_map/ppermute | solution.py:107
  796.6 6.7 collective-permute-done.49
  (447 shorter events, 253.2 us)
Async XLA Ops:
  0.7 112.3 %collective-permute-start.30 = (bf16[192,1024]{1,0:T(8,128)(2,1)}, bf16[192,1024]{1,0:T(8,128)(2,1)}, u32[]{:S(2)}, u32[]{:S(2)}) collective-permute-start(bf16[192,1024]{1,0:T(8,128)(2,1)} %bitcast.152), channel_id=1, source_target_pairs={{0,16},{1,17},{2,18},{3,19},{4,20},{5,21},{6,22},{7,23},{8,24},{9,... | collective-permute-start | bytes 1179656 | tf_op jit(solution)/shard_map/ppermute | solution.py:107
  4.8 109.7 %collective-permute-start.31 = (bf16[192,1024]{1,0:T(8,128)(2,1)}, bf16[192,1024]{1,0:T(8,128)(2,1)}, u32[]{:S(2)}, u32[]{:S(2)}) collective-permute-start(bf16[192,1024]{1,0:T(8,128)(2,1)} %bitcast.153), channel_id=1, source_target_pairs={{0,8},{1,9},{2,10},{3,11},{4,12},{5,13},{6,14},{7,15},{8,0},{9,1},... | collective-permute-start | bytes 1179656 | tf_op jit(solution)/shard_map/ppermute | solution.py:107
  26.1 90.0 %collective-permute-start.11 = (bf16[96,1536]{1,0:T(8,128)(2,1)}, bf16[96,1536]{1,0:T(8,128)(2,1)S(1)}, u32[]{:S(2)}, u32[]{:S(2)}) collective-permute-start(bf16[96,1536]{1,0:T(8,128)(2,1)} %get-tuple-element.42), channel_id=1, source_target_pairs={{0,16},{1,17},{2,18},{3,19},{4,20},{5,21},{6,22},{7,23},{8,24},{9,... | collective-permute-start | bytes 884744 | tf_op jit(solution)/shard_map/ppermute | solution.py:107
  26.5 40.8 %collective-permute-start.1 = (bf16[96,3200]{1,0:T(8,128)(2,1)S(1)}, bf16[96,3200]{1,0:T(8,128)(2,1)S(1)}, u32[]{:S(2)}, u32[]{:S(2)}) collective-permute-start(bf16[96,3200]{1,0:T(8,128)(2,1)S(1)} %pad_maximum_fusion.6), channel_id=1, source_target_pairs={{0,16},{1,17},{2,18},{3,19},{4,20},{5,21},{6,22},{7,23},{8,24},{9,... | collective-permute-start | bytes 1843208 | tf_op jit(solution)/shard_map/ppermute | solution.py:107
  38.4 34.4 %collective-permute-start.2 = (bf16[96,3200]{1,0:T(8,128)(2,1)S(1)}, bf16[96,3200]{1,0:T(8,128)(2,1)S(1)}, u32[]{:S(2)}, u32[]{:S(2)}) collective-permute-start(bf16[96,3200]{1,0:T(8,128)(2,1)S(1)} %pad_maximum_fusion.6), channel_id=1, source_target_pairs={{0,8},{1,9},{2,10},{3,11},{4,12},{5,13},{6,14},{7,15},{8,0},{9,1},... | collective-permute-start | bytes 1843208 | tf_op jit(solution)/shard_map/ppermute | solution.py:107
  67.2 17.3 %collective-permute-start.3 = (bf16[96,3200]{1,0:T(8,128)(2,1)S(1)}, bf16[96,3200]{1,0:T(8,128)(2,1)S(1)}, u32[]{:S(2)}, u32[]{:S(2)}) collective-permute-start(bf16[96,3200]{1,0:T(8,128)(2,1)S(1)} %collective-permute-done.1), channel_id=1, source_target_pairs={{0,8},{1,9},{2,10},{3,11},{4,12},{5,13},{6,14},{7,15},{8,0},{9,1},... | collective-permute-start | bytes 1843208 | tf_op jit(solution)/shard_map/ppermute | solution.py:107
  86.9 25.2 %collective-permute-start.7 = (bf16[96,3200]{1,0:T(8,128)(2,1)S(1)}, bf16[96,3200]{1,0:T(8,128)(2,1)S(1)}, u32[]{:S(2)}, u32[]{:S(2)}) collective-permute-start(bf16[96,3200]{1,0:T(8,128)(2,1)S(1)} %collective-permute-done.3), channel_id=1, source_target_pairs={{0,2},{1,3},{2,0},{3,1},{4,6},{5,7},{6,4},{7,5},{8,10},{9,11},{10,... | collective-permute-start | bytes 1843208 | tf_op jit(solution)/shard_map/ppermute | solution.py:107
  112.1 65.9 %collective-permute-start.8 = (bf16[384,3200]{1,0:T(8,128)(2,1)}, bf16[384,3200]{1,0:T(8,128)(2,1)}, u32[]{:S(2)}, u32[]{:S(2)}) collective-permute-start(bf16[384,3200]{1,0:T(8,128)(2,1)} %constant_dynamic-update-slice_fusion), channel_id=1, source_target_pairs={{0,1},{1,0},{2,3},{3,2},{4,5},{5,4},{6,7},{7,6},{8,9},{9,8},{10,11... | collective-permute-start | bytes 7372808 | tf_op jit(solution)/shard_map/ppermute | solution.py:107
  112.9 66.1 %collective-permute-start.9 = (bf16[384,3200]{1,0:T(8,128)(2,1)}, bf16[384,3200]{1,0:T(8,128)(2,1)}, u32[]{:S(2)}, u32[]{:S(2)}) collective-permute-start(bf16[384,3200]{1,0:T(8,128)(2,1)} %constant_dynamic-update-slice_fusion.5), channel_id=1, source_target_pairs={{0,1},{1,0},{2,3},{3,2},{4,5},{5,4},{6,7},{7,6},{8,9},{9,8},{10,11... | collective-permute-start | bytes 7372808 | tf_op jit(solution)/shard_map/ppermute | solution.py:107
  136.3 35.9 %collective-permute-start.23 = (bf16[192,2048]{1,0:T(8,128)(2,1)}, bf16[192,2048]{1,0:T(8,128)(2,1)S(1)}, u32[]{:S(2)}, u32[]{:S(2)}) collective-permute-start(bf16[192,2048]{1,0:T(8,128)(2,1)} %get-tuple-element.35), channel_id=1, source_target_pairs={{0,16},{1,17},{2,18},{3,19},{4,20},{5,21},{6,22},{7,23},{8,24},{9,... | collective-permute-start | bytes 2359304 | tf_op jit(solution)/shard_map/ppermute | solution.py:107
  141.3 104.0 %collective-permute-start.24 = (bf16[192,2048]{1,0:T(8,128)(2,1)}, bf16[192,2048]{1,0:T(8,128)(2,1)}, u32[]{:S(2)}, u32[]{:S(2)}) collective-permute-start(bf16[192,2048]{1,0:T(8,128)(2,1)} %get-tuple-element.35), channel_id=1, source_target_pairs={{0,8},{1,9},{2,10},{3,11},{4,12},{5,13},{6,14},{7,15},{8,0},{9,1},... | collective-permute-start | bytes 2359304 | tf_op jit(solution)/shard_map/ppermute | solution.py:107
  148.6 26.1 %collective-permute-start.17 = (bf16[96,1536]{1,0:T(8,128)(2,1)S(1)}, bf16[96,1536]{1,0:T(8,128)(2,1)S(1)}, u32[]{:S(2)}, u32[]{:S(2)}) collective-permute-start(bf16[96,1536]{1,0:T(8,128)(2,1)S(1)} %collective-permute-done.13), channel_id=1, source_target_pairs={{0,2},{1,3},{2,0},{3,1},{4,6},{5,7},{6,4},{7,5},{8,10},{9,11},{10,... | collective-permute-start | bytes 884744 | tf_op jit(solution)/shard_map/ppermute | solution.py:107
  172.3 74.5 %collective-permute-start.26 = (bf16[192,2048]{1,0:T(8,128)(2,1)}, bf16[192,2048]{1,0:T(8,128)(2,1)}, u32[]{:S(2)}, u32[]{:S(2)}) collective-permute-start(bf16[192,2048]{1,0:T(8,128)(2,1)} %get-tuple-element.35), channel_id=1, source_target_pairs={{0,4},{1,5},{2,6},{3,7},{4,0},{5,1},{6,2},{7,3},{8,12},{9,13},{10,... | collective-permute-start | bytes 2359304 | tf_op jit(solution)/shard_map/ppermute | solution.py:107
  174.7 100.4 %collective-permute-start.39 = (bf16[384,1536]{1,0:T(8,128)(2,1)}, bf16[384,1536]{1,0:T(8,128)(2,1)}, u32[]{:S(2)}, u32[]{:S(2)}) collective-permute-start(bf16[384,1536]{1,0:T(8,128)(2,1)} %fusion.57), channel_id=1, source_target_pairs={{0,2},{1,3},{2,0},{3,1},{4,6},{5,7},{6,4},{7,5},{8,10},{9,11},{10,... | collective-permute-start | bytes 3538952 | tf_op jit(solution)/shard_map/ppermute | solution.py:107
  178.0 58.2 %collective-permute-start.18 = (bf16[384,1536]{1,0:T(8,128)(2,1)}, bf16[384,1536]{1,0:T(8,128)(2,1)}, u32[]{:S(2)}, u32[]{:S(2)}) collective-permute-start(bf16[384,1536]{1,0:T(8,128)(2,1)} %constant_dynamic-update-slice_fusion.11), channel_id=1, source_target_pairs={{0,1},{1,0},{2,3},{3,2},{4,5},{5,4},{6,7},{7,6},{8,9},{9,8},{10,11... | collective-permute-start | bytes 3538952 | tf_op jit(solution)/shard_map/ppermute | solution.py:107
  179.1 59.8 %collective-permute-start.19 = (bf16[384,1536]{1,0:T(8,128)(2,1)}, bf16[384,1536]{1,0:T(8,128)(2,1)}, u32[]{:S(2)}, u32[]{:S(2)}) collective-permute-start(bf16[384,1536]{1,0:T(8,128)(2,1)} %constant_dynamic-update-slice_fusion.16), channel_id=1, source_target_pairs={{0,1},{1,0},{2,3},{3,2},{4,5},{5,4},{6,7},{7,6},{8,9},{9,8},{10,11... | collective-permute-start | bytes 3538952 | tf_op jit(solution)/shard_map/ppermute | solution.py:107
  238.9 36.3 %collective-permute-start.25 = (bf16[192,2048]{1,0:T(8,128)(2,1)S(1)}, bf16[192,2048]{1,0:T(8,128)(2,1)S(1)}, u32[]{:S(2)}, u32[]{:S(2)}) collective-permute-start(bf16[192,2048]{1,0:T(8,128)(2,1)S(1)} %copy-done.51), channel_id=1, source_target_pairs={{0,8},{1,9},{2,10},{3,11},{4,12},{5,13},{6,14},{7,15},{8,0},{9,1},... | collective-permute-start | bytes 2359304 | tf_op jit(solution)/shard_map/ppermute | solution.py:107
  245.2 30.5 %collective-permute-start.27 = (bf16[192,2048]{1,0:T(8,128)(2,1)S(1)}, bf16[192,2048]{1,0:T(8,128)(2,1)S(1)}, u32[]{:S(2)}, u32[]{:S(2)}) collective-permute-start(bf16[192,2048]{1,0:T(8,128)(2,1)S(1)} %copy-done.51), channel_id=1, source_target_pairs={{0,4},{1,5},{2,6},{3,7},{4,0},{5,1},{6,2},{7,3},{8,12},{9,13},{10,... | collective-permute-start | bytes 2359304 | tf_op jit(solution)/shard_map/ppermute | solution.py:107
  246.8 26.1 %collective-permute-start.36 = (bf16[192,1024]{1,0:T(8,128)(2,1)S(1)}, bf16[192,1024]{1,0:T(8,128)(2,1)S(1)}, u32[]{:S(2)}, u32[]{:S(2)}) collective-permute-start(bf16[192,1024]{1,0:T(8,128)(2,1)S(1)} %copy-done.62), channel_id=1, source_target_pairs={{0,4},{1,5},{2,6},{3,7},{4,0},{5,1},{6,2},{7,3},{8,12},{9,13},{10,... | collective-permute-start | bytes 1179656 | tf_op jit(solution)/shard_map/ppermute | solution.py:107
  249.6 44.0 %collective-permute-start.20 = (bf16[384,1536]{1,0:T(8,128)(2,1)S(1)}, bf16[384,1536]{1,0:T(8,128)(2,1)S(1)}, u32[]{:S(2)}, u32[]{:S(2)}) collective-permute-start(bf16[384,1536]{1,0:T(8,128)(2,1)S(1)} %fusion.47), channel_id=1, source_target_pairs={{0,2},{1,3},{2,0},{3,1},{4,6},{5,7},{6,4},{7,5},{8,10},{9,11},{10,... | collective-permute-start | bytes 3538952 | tf_op jit(solution)/shard_map/ppermute | solution.py:107
  272.9 20.7 %collective-permute-start.28 = (bf16[192,2048]{1,0:T(8,128)(2,1)}, bf16[192,2048]{1,0:T(8,128)(2,1)S(1)}, u32[]{:S(2)}, u32[]{:S(2)}) collective-permute-start(bf16[192,2048]{1,0:T(8,128)(2,1)} %collective-permute-done.24), channel_id=1, source_target_pairs={{0,4},{1,5},{2,6},{3,7},{4,0},{5,1},{6,2},{7,3},{8,12},{9,13},{10,... | collective-permute-start | bytes 2359304 | tf_op jit(solution)/shard_map/ppermute | solution.py:107
  275.2 34.0 %collective-permute-start.40 = (bf16[384,1536]{1,0:T(8,128)(2,1)}, bf16[384,1536]{1,0:T(8,128)(2,1)S(1)}, u32[]{:S(2)}, u32[]{:S(2)}) collective-permute-start(bf16[384,1536]{1,0:T(8,128)(2,1)} %fusion.57), channel_id=1, source_target_pairs={{0,1},{1,0},{2,3},{3,2},{4,5},{5,4},{6,7},{7,6},{8,9},{9,8},{10,11... | collective-permute-start | bytes 3538952 | tf_op jit(solution)/shard_map/ppermute | solution.py:107
  275.2 34.0 %collective-permute-start.41 = (bf16[384,1536]{1,0:T(8,128)(2,1)}, bf16[384,1536]{1,0:T(8,128)(2,1)S(1)}, u32[]{:S(2)}, u32[]{:S(2)}) collective-permute-start(bf16[384,1536]{1,0:T(8,128)(2,1)} %collective-permute-done.39), channel_id=1, source_target_pairs={{0,1},{1,0},{2,3},{3,2},{4,5},{5,4},{6,7},{7,6},{8,9},{9,8},{10,11... | collective-permute-start | bytes 3538952 | tf_op jit(solution)/shard_map/ppermute | solution.py:107
  275.7 32.6 %collective-permute-start.29 = (bf16[192,2048]{1,0:T(8,128)(2,1)S(1)}, bf16[192,2048]{1,0:T(8,128)(2,1)S(1)}, u32[]{:S(2)}, u32[]{:S(2)}) collective-permute-start(bf16[192,2048]{1,0:T(8,128)(2,1)S(1)} %collective-permute-done.25), channel_id=1, source_target_pairs={{0,4},{1,5},{2,6},{3,7},{4,0},{5,1},{6,2},{7,3},{8,12},{9,13},{10,... | collective-permute-start | bytes 2359304 | tf_op jit(solution)/shard_map/ppermute | solution.py:107
  293.6 18.3 %collective-permute-start.21 = (bf16[384,1536]{1,0:T(8,128)(2,1)S(1)}, bf16[384,1536]{1,0:T(8,128)(2,1)S(1)}, u32[]{:S(2)}, u32[]{:S(2)}) collective-permute-start(bf16[384,1536]{1,0:T(8,128)(2,1)S(1)} %fusion.47), channel_id=1, source_target_pairs={{0,1},{1,0},{2,3},{3,2},{4,5},{5,4},{6,7},{7,6},{8,9},{9,8},{10,11... | collective-permute-start | bytes 3538952 | tf_op jit(solution)/shard_map/ppermute | solution.py:107
  293.6 18.4 %collective-permute-start.22 = (bf16[384,1536]{1,0:T(8,128)(2,1)S(1)}, bf16[384,1536]{1,0:T(8,128)(2,1)S(1)}, u32[]{:S(2)}, u32[]{:S(2)}) collective-permute-start(bf16[384,1536]{1,0:T(8,128)(2,1)S(1)} %collective-permute-done.20), channel_id=1, source_target_pairs={{0,1},{1,0},{2,3},{3,2},{4,5},{5,4},{6,7},{7,6},{8,9},{9,8},{10,11... | collective-permute-start | bytes 3538952 | tf_op jit(solution)/shard_map/ppermute | solution.py:107
  352.7 37.6 %collective-permute-start.62 = (bf16[768,1024]{1,0:T(8,128)(2,1)}, bf16[768,1024]{1,0:T(8,128)(2,1)}, u32[]{:S(2)}, u32[]{:S(2)}) collective-permute-start(bf16[768,1024]{1,0:T(8,128)(2,1)} %fusion.92), channel_id=1, source_target_pairs={{0,4},{1,5},{2,6},{3,7},{4,0},{5,1},{6,2},{7,3},{8,12},{9,13},{10,... | collective-permute-start | bytes 4718600 | tf_op jit(solution)/shard_map/ppermute | solution.py:107
  358.3 65.7 %collective-permute-start.59 = (bf16[768,1024]{1,0:T(8,128)(2,1)}, bf16[768,1024]{1,0:T(8,128)(2,1)}, u32[]{:S(2)}, u32[]{:S(2)}) collective-permute-start(bf16[768,1024]{1,0:T(8,128)(2,1)} %fusion.89), channel_id=1, source_target_pairs={{0,4},{1,5},{2,6},{3,7},{4,0},{5,1},{6,2},{7,3},{8,12},{9,13},{10,... | collective-permute-start | bytes 4718600 | tf_op jit(solution)/shard_map/ppermute | solution.py:107
  378.7 75.8 %collective-permute-start.56 = (bf16[768,1024]{1,0:T(8,128)(2,1)}, bf16[768,1024]{1,0:T(8,128)(2,1)S(1)}, u32[]{:S(2)}, u32[]{:S(2)}) collective-permute-start(bf16[768,1024]{1,0:T(8,128)(2,1)} %fusion.86), channel_id=1, source_target_pairs={{0,4},{1,5},{2,6},{3,7},{4,0},{5,1},{6,2},{7,3},{8,12},{9,13},{10,... | collective-permute-start | bytes 4718600 | tf_op jit(solution)/shard_map/ppermute | solution.py:107
  386.8 100.3 %collective-permute-start.42 = (bf16[768,1536]{1,0:T(8,128)(2,1)S(1)}, bf16[768,1536]{1,0:T(8,128)(2,1)}, u32[]{:S(2)}, u32[]{:S(2)}) collective-permute-start(bf16[768,1536]{1,0:T(8,128)(2,1)S(1)} %slice.327), channel_id=1, source_target_pairs={{0,1},{1,0},{2,3},{3,2},{4,5},{5,4},{6,7},{7,6},{8,9},{9,8},{10,11... | collective-permute-start | bytes 7077896 | tf_op jit(solution)/shard_map/ppermute | solution.py:107
  387.1 104.6 %collective-permute-start.37 = (bf16[768,1536]{1,0:T(8,128)(2,1)S(1)}, bf16[768,1536]{1,0:T(8,128)(2,1)}, u32[]{:S(2)}, u32[]{:S(2)}) collective-permute-start(bf16[768,1536]{1,0:T(8,128)(2,1)S(1)} %slice.323), channel_id=1, source_target_pairs={{0,1},{1,0},{2,3},{3,2},{4,5},{5,4},{6,7},{7,6},{8,9},{9,8},{10,11... | collective-permute-start | bytes 7077896 | tf_op jit(solution)/shard_map/ppermute | solution.py:107
  394.6 64.4 %collective-permute-start.63 = (bf16[384,1024]{1,0:T(8,128)(2,1)S(1)}, bf16[384,1024]{1,0:T(8,128)(2,1)S(1)}, u32[]{:S(2)}, u32[]{:S(2)}) collective-permute-start(bf16[384,1024]{1,0:T(8,128)(2,1)S(1)} %slice.497), channel_id=1, source_target_pairs={{0,8},{1,9},{2,10},{3,11},{4,12},{5,13},{6,14},{7,15},{8,0},{9,1},... | collective-permute-start | bytes 2359304 | tf_op jit(solution)/shard_map/ppermute | solution.py:107
  428.3 32.3 %collective-permute-start.60 = (bf16[384,1024]{1,0:T(8,128)(2,1)S(1)}, bf16[384,1024]{1,0:T(8,128)(2,1)S(1)}, u32[]{:S(2)}, u32[]{:S(2)}) collective-permute-start(bf16[384,1024]{1,0:T(8,128)(2,1)S(1)} %slice.498), channel_id=1, source_target_pairs={{0,8},{1,9},{2,10},{3,11},{4,12},{5,13},{6,14},{7,15},{8,0},{9,1},... | collective-permute-start | bytes 2359304 | tf_op jit(solution)/shard_map/ppermute | solution.py:107
  457.4 29.1 %collective-permute-start.57 = (bf16[384,1024]{1,0:T(8,128)(2,1)S(1)}, bf16[384,1024]{1,0:T(8,128)(2,1)S(1)}, u32[]{:S(2)}, u32[]{:S(2)}) collective-permute-start(bf16[384,1024]{1,0:T(8,128)(2,1)S(1)} %slice.499), channel_id=1, source_target_pairs={{0,8},{1,9},{2,10},{3,11},{4,12},{5,13},{6,14},{7,15},{8,0},{9,1},... | collective-permute-start | bytes 2359304 | tf_op jit(solution)/shard_map/ppermute | solution.py:107
  460.2 83.6 %collective-permute-start.64 = (bf16[192,1024]{1,0:T(8,128)(2,1)}, bf16[192,1024]{1,0:T(8,128)(2,1)}, u32[]{:S(2)}, u32[]{:S(2)}) collective-permute-start(bf16[192,1024]{1,0:T(8,128)(2,1)} %slice.503), channel_id=1, source_target_pairs={{0,16},{1,17},{2,18},{3,19},{4,20},{5,21},{6,22},{7,23},{8,24},{9,... | collective-permute-start | bytes 1179656 | tf_op jit(solution)/shard_map/ppermute | solution.py:107
  460.9 45.7 %collective-permute-start.61 = (bf16[192,1024]{1,0:T(8,128)(2,1)S(1)}, bf16[192,1024]{1,0:T(8,128)(2,1)S(1)}, u32[]{:S(2)}, u32[]{:S(2)}) collective-permute-start(bf16[192,1024]{1,0:T(8,128)(2,1)S(1)} %slice.504), channel_id=1, source_target_pairs={{0,16},{1,17},{2,18},{3,19},{4,20},{5,21},{6,22},{7,23},{8,24},{9,... | collective-permute-start | bytes 1179656 | tf_op jit(solution)/shard_map/ppermute | solution.py:107
  486.7 24.1 %collective-permute-start.58 = (bf16[192,1024]{1,0:T(8,128)(2,1)S(1)}, bf16[192,1024]{1,0:T(8,128)(2,1)S(1)}, u32[]{:S(2)}, u32[]{:S(2)}) collective-permute-start(bf16[192,1024]{1,0:T(8,128)(2,1)S(1)} %slice.505), channel_id=1, source_target_pairs={{0,16},{1,17},{2,18},{3,19},{4,20},{5,21},{6,22},{7,23},{8,24},{9,... | collective-permute-start | bytes 1179656 | tf_op jit(solution)/shard_map/ppermute | solution.py:107
  489.6 56.4 %collective-permute-start.43 = (bf16[384,1536]{1,0:T(8,128)(2,1)S(1)}, bf16[384,1536]{1,0:T(8,128)(2,1)}, u32[]{:S(2)}, u32[]{:S(2)}) collective-permute-start(bf16[384,1536]{1,0:T(8,128)(2,1)S(1)} %slice.495), channel_id=1, source_target_pairs={{0,2},{1,3},{2,0},{3,1},{4,6},{5,7},{6,4},{7,5},{8,10},{9,11},{10,... | collective-permute-start | bytes 3538952 | tf_op jit(solution)/shard_map/ppermute | solution.py:107
  495.3 272.0 %collective-permute-start.38 = (bf16[384,1536]{1,0:T(8,128)(2,1)}, bf16[384,1536]{1,0:T(8,128)(2,1)}, u32[]{:S(2)}, u32[]{:S(2)}) collective-permute-start(bf16[384,1536]{1,0:T(8,128)(2,1)} %slice.496), channel_id=1, source_target_pairs={{0,2},{1,3},{2,0},{3,1},{4,6},{5,7},{6,4},{7,5},{8,10},{9,11},{10,... | collective-permute-start | bytes 3538952 | tf_op jit(solution)/shard_map/ppermute | solution.py:107
  624.0 25.9 %collective-permute-start.50 = (bf16[384,1536]{1,0:T(8,128)(2,1)S(1)}, bf16[384,1536]{1,0:T(8,128)(2,1)S(1)}, u32[]{:S(2)}, u32[]{:S(2)}) collective-permute-start(bf16[384,1536]{1,0:T(8,128)(2,1)S(1)} %copy-done.47), channel_id=1, source_target_pairs={{0,1},{1,0},{2,3},{3,2},{4,5},{5,4},{6,7},{7,6},{8,9},{9,8},{10,11... | collective-permute-start | bytes 3538952 | tf_op jit(solution)/shard_map/ppermute | solution.py:107
  624.2 17.5 %collective-permute-start.51 = (bf16[384,1536]{1,0:T(8,128)(2,1)S(1)}, bf16[384,1536]{1,0:T(8,128)(2,1)S(1)}, u32[]{:S(2)}, u32[]{:S(2)}) collective-permute-start(bf16[384,1536]{1,0:T(8,128)(2,1)S(1)} %convolution_convert_fusion.4), channel_id=1, source_target_pairs={{0,1},{1,0},{2,3},{3,2},{4,5},{5,4},{6,7},{7,6},{8,9},{9,8},{10,11... | collective-permute-start | bytes 3538952 | tf_op jit(solution)/shard_map/ppermute | solution.py:107
  625.9 95.8 %collective-permute-start.44 = (bf16[384,3072]{1,0:T(8,128)(2,1)S(1)}, bf16[384,3072]{1,0:T(8,128)(2,1)S(1)}, u32[]{:S(2)}, u32[]{:S(2)}) collective-permute-start(bf16[384,3072]{1,0:T(8,128)(2,1)S(1)} %convolution_convert_fusion.3), channel_id=1, source_target_pairs={{0,1},{1,0},{2,3},{3,2},{4,5},{5,4},{6,7},{7,6},{8,9},{9,8},{10,11... | collective-permute-start | bytes 7077896 | tf_op jit(solution)/shard_map/ppermute | solution.py:107
  640.7 80.9 %collective-permute-start.46 = (bf16[384,3072]{1,0:T(8,128)(2,1)S(1)}, bf16[384,3072]{1,0:T(8,128)(2,1)S(1)}, u32[]{:S(2)}, u32[]{:S(2)}) collective-permute-start(bf16[384,3072]{1,0:T(8,128)(2,1)S(1)} %add_convert_fusion), channel_id=1, source_target_pairs={{0,2},{1,3},{2,0},{3,1},{4,6},{5,7},{6,4},{7,5},{8,10},{9,11},{10,... | collective-permute-start | bytes 7077896 | tf_op jit(solution)/shard_map/ppermute | solution.py:107
  642.5 77.0 %collective-permute-start.52 = (bf16[384,1536]{1,0:T(8,128)(2,1)S(1)}, bf16[384,1536]{1,0:T(8,128)(2,1)S(1)}, u32[]{:S(2)}, u32[]{:S(2)}) collective-permute-start(bf16[384,1536]{1,0:T(8,128)(2,1)S(1)} %add_convert_fusion.3), channel_id=1, source_target_pairs={{0,2},{1,3},{2,0},{3,1},{4,6},{5,7},{6,4},{7,5},{8,10},{9,11},{10,... | collective-permute-start | bytes 3538952 | tf_op jit(solution)/shard_map/ppermute | solution.py:107
  723.0 43.4 %collective-permute-start.47 = (bf16[192,3072]{1,0:T(8,128)(2,1)S(1)}, bf16[192,3072]{1,0:T(8,128)(2,1)S(1)}, u32[]{:S(2)}, u32[]{:S(2)}) collective-permute-start(bf16[192,3072]{1,0:T(8,128)(2,1)S(1)} %slice.494), channel_id=1, source_target_pairs={{0,8},{1,9},{2,10},{3,11},{4,12},{5,13},{6,14},{7,15},{8,0},{9,1},... | collective-permute-start | bytes 3538952 | tf_op jit(solution)/shard_map/ppermute | solution.py:107
  736.5 35.3 %collective-permute-start.54 = (bf16[96,1536]{1,0:T(8,128)(2,1)S(1)}, bf16[96,1536]{1,0:T(8,128)(2,1)S(1)}, u32[]{:S(2)}, u32[]{:S(2)}) collective-permute-start(bf16[96,1536]{1,0:T(8,128)(2,1)S(1)} %slice.506), channel_id=1, source_target_pairs={{0,16},{1,17},{2,18},{3,19},{4,20},{5,21},{6,22},{7,23},{8,24},{9,... | collective-permute-start | bytes 884744 | tf_op jit(solution)/shard_map/ppermute | solution.py:107
  766.8 27.4 %collective-permute-start.48 = (bf16[96,3072]{1,0:T(8,128)(2,1)S(1)}, bf16[96,3072]{1,0:T(8,128)(2,1)S(1)}, u32[]{:S(2)}, u32[]{:S(2)}) collective-permute-start(bf16[96,3072]{1,0:T(8,128)(2,1)S(1)} %slice.501), channel_id=1, source_target_pairs={{0,16},{1,17},{2,18},{3,19},{4,20},{5,21},{6,22},{7,23},{8,24},{9,... | collective-permute-start | bytes 1769480 | tf_op jit(solution)/shard_map/ppermute | solution.py:107
  772.0 23.8 %collective-permute-start.55 = (bf16[48,1536]{1,0:T(8,128)(2,1)S(1)}, bf16[48,1536]{1,0:T(8,128)(2,1)S(1)}, u32[]{:S(2)}, u32[]{:S(2)}) collective-permute-start(bf16[48,1536]{1,0:T(8,128)(2,1)S(1)} %slice.508), channel_id=1, source_target_pairs={{0,4},{1,5},{2,6},{3,7},{4,0},{5,1},{6,2},{7,3},{8,12},{9,13},{10,... | collective-permute-start | bytes 442376 | tf_op jit(solution)/shard_map/ppermute | solution.py:107
  (100 other events, 1741.5 us)
where the time goes:
time: 816 us; the launch traced here: 806 us
  waiting for transfers between devices  386 us (47%)
  matrix products  181 us (22%)
  local copies, waits for them, and re-layouts  104 us (13%)
  starting transfers between devices  59.2 us (7%)
  other arithmetic  43.3 us (5%)
  blocking collectives  29.6 us (4%)
    ppermute x65, waiting for transfers between devices, swap(): return lax.ppermute(array, AXES, [(i, i ^ mask) for i in range(world)])  386 us
    dot_general x16, matrix products, against(): lax.dot_general(left_side, right_side, (((1,), (1,)), ((), ())), preferre...  67.4 us
    dot_general x14, matrix products, product(): return jnp.dot(left_side, right_side, preferred_element_type=f32)  66.6 us
    ppermute x65, starting transfers between devices, swap(): return lax.ppermute(array, AXES, [(i, i ^ mask) for i in range(world)])  59.2 us
    unnamed x201, local copies, waits for them, and re-layouts  42.8 us
    dot_general x14, matrix products, across(): lax.dot_general(left_side, right_side, (((0,), (0,)), ((), ())), preferre...  36.2 us
    psum x1, blocking collectives, per_device(): second = lax.psum(second, 'tensor')  29.6 us
  transfers between devices with their start and end apart: 65, of which 26 were waited for; matrix products, arithmetic and copies ran while one was open for 35% of the time, Pallas kernels for 0%

commit v1 on v0

--- a/solution.py
+++ b/solution.py
@@ -308,7 +308,7 @@
         second = jnp.sum(
             gate_weight.astype(f32) * gate_grad + up_weight.astype(f32) * up_grad, axis=1
         )
-        second = lax.psum(second, "tensor")
+        second = jnp.sum(lax.all_gather(second, "tensor"), axis=0)
         second = lax.dynamic_slice(second, (t_i * shard,), (shard,))
         second_gain_grad = second / second_gain.astype(f32)
         return (

time: 816 us -> 817 us (level)
    psum x1 -> x0, blocking collectives: 29.6 us -> none  [per_device(): second = lax.psum(second, 'tensor')]
    unnamed x0 -> x1, blocking collectives: none -> 29.6 us
    unnamed x201 -> x210, local copies, waits for them, and re-layouts: 42.8 us -> 43.5 us
where the time goes in v1:
time: 817 us; the launch traced here: 807 us
  waiting for transfers between devices  386 us (47%)
  matrix products  181 us (22%)
  local copies, waits for them, and re-layouts  104 us (13%)
  starting transfers between devices  59.6 us (7%)
  other arithmetic  42.7 us (5%)
  blocking collectives  29.6 us (4%)
    ppermute x65, waiting for transfers between devices, swap(): return lax.ppermute(array, AXES, [(i, i ^ mask) for i in range(world)])  386 us
    dot_general x16, matrix products, against(): lax.dot_general(left_side, right_side, (((1,), (1,)), ((), ())), preferre...  67.4 us
    dot_general x14, matrix products, product(): return jnp.dot(left_side, right_side, preferred_element_type=f32)  66.6 us
    ppermute x65, starting transfers between devices, swap(): return lax.ppermute(array, AXES, [(i, i ^ mask) for i in range(world)])  59.6 us
    unnamed x210, local copies, waits for them, and re-layouts  43.5 us
    dot_general x14, matrix products, across(): lax.dot_general(left_side, right_side, (((0,), (0,)), ((), ())), preferre...  36.2 us
    unnamed x1, blocking collectives  29.6 us
  transfers between devices with their start and end apart: 65, of which 26 were waited for; matrix products, arithmetic and copies ran while one was open for 35% of the time, Pallas kernels for 0%

profile of v1, /device:TPU:0, one launch (start us, length us, event | category | flops | bytes accessed | tf_op | source)
XLA Modules:
  0.0 806.7 jit_solution(12888782083300831156)
XLA Ops:
  0.7 4.1 collective-permute-start.30
  31.1 8.6 %collective-permute-done.4 = bf16[96,3200]{1,0:T(8,128)(2,1)S(1)} collective-permute-done((bf16[96,3200]{1,0:T(8,128)(2,1)S(1)}, bf16[96,3200]{1,0:T(8,128)(2,1)S(1)}, u32[]{:S(2)}, u32[]{:S(2)}) %collective-permute-start.4) | collective-permute-done | bytes 614432 | tf_op jit(solution)/shard_map/ppermute | solution.py:107
  41.0 27.5 %collective-permute-done.1 = bf16[96,3200]{1,0:T(8,128)(2,1)S(1)} collective-permute-done((bf16[96,3200]{1,0:T(8,128)(2,1)S(1)}, bf16[96,3200]{1,0:T(8,128)(2,1)S(1)}, u32[]{:S(2)}, u32[]{:S(2)}) %collective-permute-start.1) | collective-permute-done | bytes 614432 | tf_op jit(solution)/shard_map/ppermute | solution.py:107
  69.4 4.7 collective-permute-done.2
  77.4 8.4 %collective-permute-done.3 = bf16[96,3200]{1,0:T(8,128)(2,1)S(1)} collective-permute-done((bf16[96,3200]{1,0:T(8,128)(2,1)S(1)}, bf16[96,3200]{1,0:T(8,128)(2,1)S(1)}, u32[]{:S(2)}, u32[]{:S(2)}) %collective-permute-start.3) | collective-permute-done | bytes 614432 | tf_op jit(solution)/shard_map/ppermute | solution.py:107
  89.6 13.0 %collective-permute-done.6 = bf16[96,3200]{1,0:T(8,128)(2,1)S(1)} collective-permute-done((bf16[96,3200]{1,0:T(8,128)(2,1)S(1)}, bf16[96,3200]{1,0:T(8,128)(2,1)S(1)}, u32[]{:S(2)}, u32[]{:S(2)}) %collective-permute-start.6) | collective-permute-done | bytes 614432 | tf_op jit(solution)/shard_map/ppermute | solution.py:107
  103.4 9.9 %collective-permute-done.7 = bf16[96,3200]{1,0:T(8,128)(2,1)S(1)} collective-permute-done((bf16[96,3200]{1,0:T(8,128)(2,1)S(1)}, bf16[96,3200]{1,0:T(8,128)(2,1)S(1)}, u32[]{:S(2)}, u32[]{:S(2)}) %collective-permute-start.7) | collective-permute-done | bytes 614432 | tf_op jit(solution)/shard_map/ppermute | solution.py:107
  120.4 5.5 collective-permute-done.14
  128.0 4.3 collective-permute-done.15
  133.8 3.8 collective-permute-done.16
  142.6 7.3 collective-permute-done.34
  150.5 23.1 %collective-permute-done.23 = bf16[192,2048]{1,0:T(8,128)(2,1)S(1)} collective-permute-done((bf16[192,2048]{1,0:T(8,128)(2,1)}, bf16[192,2048]{1,0:T(8,128)(2,1)S(1)}, u32[]{:S(2)}, u32[]{:S(2)}) %collective-permute-start.23) | collective-permute-done | bytes 786464 | tf_op jit(solution)/shard_map/ppermute | solution.py:107
  182.0 4.3 multiply_convert_fusion.4
  186.3 3.6 fusion.149
  189.9 3.7 fusion.137
  212.2 3.7 subtract_convert_fusion.1
  255.3 18.8 %collective-permute-done.36 = bf16[192,1024]{1,0:T(8,128)(2,1)S(1)} collective-permute-done((bf16[192,1024]{1,0:T(8,128)(2,1)S(1)}, bf16[192,1024]{1,0:T(8,128)(2,1)S(1)}, u32[]{:S(2)}, u32[]{:S(2)}) %collective-permute-start.36) | collective-permute-done | bytes 393248 | tf_op jit(solution)/shard_map/ppermute | solution.py:107
  281.5 13.4 %collective-permute-done.28 = bf16[192,2048]{1,0:T(8,128)(2,1)S(1)} collective-permute-done((bf16[192,2048]{1,0:T(8,128)(2,1)}, bf16[192,2048]{1,0:T(8,128)(2,1)S(1)}, u32[]{:S(2)}, u32[]{:S(2)}) %collective-permute-start.28) | collective-permute-done | bytes 786464 | tf_op jit(solution)/shard_map/ppermute | solution.py:107
  296.3 13.2 %collective-permute-done.29 = bf16[192,2048]{1,0:T(8,128)(2,1)S(1)} collective-permute-done((bf16[192,2048]{1,0:T(8,128)(2,1)S(1)}, bf16[192,2048]{1,0:T(8,128)(2,1)S(1)}, u32[]{:S(2)}, u32[]{:S(2)}) %collective-permute-start.29) | collective-permute-done | bytes 786464 | tf_op jit(solution)/shard_map/ppermute | solution.py:107
  315.3 16.8 %fusion.176 = f32[1536,2048]{1,0:T(8,128)} fusion(bf16[1536,2048]{1,0:T(8,128)(2,1)S(1)} %copy-done.68, bf16[384,1536]{1,0:T(8,128)(2,1)S(1)} %collective-permute-done.22, bf16[384,1536]{1,0:T(8,128)(2,1)S(1)} %collective-permute-done.21, bf16[384,1536]{1,0:T(8,128)(2,1)S(1)} %collective-permute-done.20, bf16[384,1536]{1,0:T(8,128)(2,1)S(1)} %fusion.47), kind=kOutput, calls=%fused_computation.319 | convolution fusion | flops 9682550784 | bytes 23592960 | tf_op jit(solution)/shard_map/dot_general | solution.py:55
  332.1 15.0 %multiply_convert_fusion.1 = (bf16[1536,1024]{1,0:T(8,128)(2,1)S(1)}, bf16[1536,1024]{1,0:T(8,128)(2,1)}, bf16[1536,1024]{1,0:T(8,128)(2,1)}) fusion(f32[1536,2048]{1,0:T(8,128)} %fusion.176, bf16[1536,1024]{1,0:T(8,128)(2,1)} %constant_dynamic-update-slice_fusion.31, bf16[384,1536]{1,0:T(8,128)(2,1)} %copy-done.42, bf16[384,1536]{1,0:T(8,128)(2,1)} %copy-done.41, ...), kind=kOutput, calls=%fused_computation.19 | convolution fusion | flops 4875878400 | bytes 29884416 | tf_op jit(solution)/shard_map/dot_general | solution.py:55
  347.1 6.8 fusion.92
  355.8 3.8 fusion.89
  361.1 15.1 %convolution_convert_fusion.1 = bf16[1536,1536]{1,0:T(8,128)(2,1)} fusion(bf16[1536,2048]{1,0:T(8,128)(2,1)} %constant_dynamic-update-slice_fusion.22, bf16[1536,1024]{1,0:T(8,128)(2,1)} %get-tuple-element.19, bf16[1536,1024]{1,0:T(8,128)(2,1)S(1)} %get-tuple-element.18), kind=kOutput, calls=%fused_computation.14 | convolution fusion | flops 9678618624 | bytes 17301504 | tf_op jit(solution)/shard_map/dot_general | solution.py:65
  376.2 3.8 fusion.86
  380.6 7.4 convolution_convert_fusion
  391.6 4.2 convert_add_fusion.3
  397.3 28.0 %collective-permute-done.59 = bf16[768,1024]{1,0:T(8,128)(2,1)} collective-permute-done((bf16[768,1024]{1,0:T(8,128)(2,1)}, bf16[768,1024]{1,0:T(8,128)(2,1)}, u32[]{:S(2)}, u32[]{:S(2)}) %collective-permute-start.59) | collective-permute-done | bytes 1572896 | tf_op jit(solution)/shard_map/ppermute | solution.py:107
  425.3 4.1 convert_add_fusion.4
  431.0 24.9 %collective-permute-done.56 = bf16[768,1024]{1,0:T(8,128)(2,1)S(1)} collective-permute-done((bf16[768,1024]{1,0:T(8,128)(2,1)}, bf16[768,1024]{1,0:T(8,128)(2,1)S(1)}, u32[]{:S(2)}, u32[]{:S(2)}) %collective-permute-start.56) | collective-permute-done | bytes 1572896 | tf_op jit(solution)/shard_map/ppermute | solution.py:107
  464.9 22.8 %collective-permute-done.57 = bf16[384,1024]{1,0:T(8,128)(2,1)S(1)} collective-permute-done((bf16[384,1024]{1,0:T(8,128)(2,1)S(1)}, bf16[384,1024]{1,0:T(8,128)(2,1)S(1)}, u32[]{:S(2)}, u32[]{:S(2)}) %collective-permute-start.57) | collective-permute-done | bytes 786464 | tf_op jit(solution)/shard_map/ppermute | solution.py:107
  498.0 10.0 %collective-permute-done.61 = bf16[192,1024]{1,0:T(8,128)(2,1)S(1)} collective-permute-done((bf16[192,1024]{1,0:T(8,128)(2,1)S(1)}, bf16[192,1024]{1,0:T(8,128)(2,1)S(1)}, u32[]{:S(2)}, u32[]{:S(2)}) %collective-permute-start.61) | collective-permute-done | bytes 393248 | tf_op jit(solution)/shard_map/ppermute | solution.py:107
  508.0 4.2 collective-permute-done.58
  513.8 29.6 %all-reduce.1 = f32[768]{0:T(1024)S(1)} all-reduce(f32[768]{0:T(1024)S(1)} %dynamic-update-slice), channel_id=2, replica_groups=mesh['dp'=8,'tensor'=4] {'tensor'}, use_global_device_ids=true, to_apply=%add.1 | all-reduce | flops 768 | bytes 6144
  547.0 4.5 multiply_reduce_fusion.1
  567.9 6.6 reshape.247
  574.5 4.8 copy.140
  579.3 3.8 fusion.102
  610.5 3.7 subtract_convert_fusion
  616.2 4.1 convert_element_type.310
  646.4 4.4 fusion.5
  650.8 69.7 %collective-permute-done.52 = bf16[384,1536]{1,0:T(8,128)(2,1)S(1)} collective-permute-done((bf16[384,1536]{1,0:T(8,128)(2,1)S(1)}, bf16[384,1536]{1,0:T(8,128)(2,1)S(1)}, u32[]{:S(2)}, u32[]{:S(2)}) %collective-permute-start.52) | collective-permute-done | bytes 1179680 | tf_op jit(solution)/shard_map/ppermute | solution.py:107
  725.4 6.1 fusion.40
  731.5 5.8 collective-permute-done.53
  740.2 27.2 %collective-permute-done.47 = bf16[192,3072]{1,0:T(8,128)(2,1)S(1)} collective-permute-done((bf16[192,3072]{1,0:T(8,128)(2,1)S(1)}, bf16[192,3072]{1,0:T(8,128)(2,1)S(1)}, u32[]{:S(2)}, u32[]{:S(2)}) %collective-permute-start.47) | collective-permute-done | bytes 1179680 | tf_op jit(solution)/shard_map/ppermute | solution.py:107
  768.3 4.6 fusion.49
  774.6 20.6 %collective-permute-done.48 = bf16[96,3072]{1,0:T(8,128)(2,1)S(1)} collective-permute-done((bf16[96,3072]{1,0:T(8,128)(2,1)S(1)}, bf16[96,3072]{1,0:T(8,128)(2,1)S(1)}, u32[]{:S(2)}, u32[]{:S(2)}) %collective-permute-start.48) | collective-permute-done | bytes 589856 | tf_op jit(solution)/shard_map/ppermute | solution.py:107
  797.7 6.6 collective-permute-done.49
  (458 shorter events, 253.8 us)
Async XLA Ops:
  0.7 113.6 %collective-permute-start.30 = (bf16[192,1024]{1,0:T(8,128)(2,1)}, bf16[192,1024]{1,0:T(8,128)(2,1)}, u32[]{:S(2)}, u32[]{:S(2)}) collective-permute-start(bf16[192,1024]{1,0:T(8,128)(2,1)} %bitcast.153), channel_id=1, source_target_pairs={{0,16},{1,17},{2,18},{3,19},{4,20},{5,21},{6,22},{7,23},{8,24},{9,... | collective-permute-start | bytes 1179656 | tf_op jit(solution)/shard_map/ppermute | solution.py:107
  4.8 111.0 %collective-permute-start.31 = (bf16[192,1024]{1,0:T(8,128)(2,1)}, bf16[192,1024]{1,0:T(8,128)(2,1)}, u32[]{:S(2)}, u32[]{:S(2)}) collective-permute-start(bf16[192,1024]{1,0:T(8,128)(2,1)} %bitcast.154), channel_id=1, source_target_pairs={{0,8},{1,9},{2,10},{3,11},{4,12},{5,13},{6,14},{7,15},{8,0},{9,1},... | collective-permute-start | bytes 1179656 | tf_op jit(solution)/shard_map/ppermute | solution.py:107
  27.4 90.0 %collective-permute-start.11 = (bf16[96,1536]{1,0:T(8,128)(2,1)}, bf16[96,1536]{1,0:T(8,128)(2,1)S(1)}, u32[]{:S(2)}, u32[]{:S(2)}) collective-permute-start(bf16[96,1536]{1,0:T(8,128)(2,1)} %get-tuple-element.42), channel_id=1, source_target_pairs={{0,16},{1,17},{2,18},{3,19},{4,20},{5,21},{6,22},{7,23},{8,24},{9,... | collective-permute-start | bytes 884744 | tf_op jit(solution)/shard_map/ppermute | solution.py:107
  27.8 40.8 %collective-permute-start.1 = (bf16[96,3200]{1,0:T(8,128)(2,1)S(1)}, bf16[96,3200]{1,0:T(8,128)(2,1)S(1)}, u32[]{:S(2)}, u32[]{:S(2)}) collective-permute-start(bf16[96,3200]{1,0:T(8,128)(2,1)S(1)} %pad_maximum_fusion.6), channel_id=1, source_target_pairs={{0,16},{1,17},{2,18},{3,19},{4,20},{5,21},{6,22},{7,23},{8,24},{9,... | collective-permute-start | bytes 1843208 | tf_op jit(solution)/shard_map/ppermute | solution.py:107
  39.7 34.4 %collective-permute-start.2 = (bf16[96,3200]{1,0:T(8,128)(2,1)S(1)}, bf16[96,3200]{1,0:T(8,128)(2,1)S(1)}, u32[]{:S(2)}, u32[]{:S(2)}) collective-permute-start(bf16[96,3200]{1,0:T(8,128)(2,1)S(1)} %pad_maximum_fusion.6), channel_id=1, source_target_pairs={{0,8},{1,9},{2,10},{3,11},{4,12},{5,13},{6,14},{7,15},{8,0},{9,1},... | collective-permute-start | bytes 1843208 | tf_op jit(solution)/shard_map/ppermute | solution.py:107
  68.5 17.3 %collective-permute-start.3 = (bf16[96,3200]{1,0:T(8,128)(2,1)S(1)}, bf16[96,3200]{1,0:T(8,128)(2,1)S(1)}, u32[]{:S(2)}, u32[]{:S(2)}) collective-permute-start(bf16[96,3200]{1,0:T(8,128)(2,1)S(1)} %collective-permute-done.1), channel_id=1, source_target_pairs={{0,8},{1,9},{2,10},{3,11},{4,12},{5,13},{6,14},{7,15},{8,0},{9,1},... | collective-permute-start | bytes 1843208 | tf_op jit(solution)/shard_map/ppermute | solution.py:107
  88.1 25.2 %collective-permute-start.7 = (bf16[96,3200]{1,0:T(8,128)(2,1)S(1)}, bf16[96,3200]{1,0:T(8,128)(2,1)S(1)}, u32[]{:S(2)}, u32[]{:S(2)}) collective-permute-start(bf16[96,3200]{1,0:T(8,128)(2,1)S(1)} %collective-permute-done.3), channel_id=1, source_target_pairs={{0,2},{1,3},{2,0},{3,1},{4,6},{5,7},{6,4},{7,5},{8,10},{9,11},{10,... | collective-permute-start | bytes 1843208 | tf_op jit(solution)/shard_map/ppermute | solution.py:107
  113.3 65.9 %collective-permute-start.8 = (bf16[384,3200]{1,0:T(8,128)(2,1)}, bf16[384,3200]{1,0:T(8,128)(2,1)}, u32[]{:S(2)}, u32[]{:S(2)}) collective-permute-start(bf16[384,3200]{1,0:T(8,128)(2,1)} %constant_dynamic-update-slice_fusion), channel_id=1, source_target_pairs={{0,1},{1,0},{2,3},{3,2},{4,5},{5,4},{6,7},{7,6},{8,9},{9,8},{10,11... | collective-permute-start | bytes 7372808 | tf_op jit(solution)/shard_map/ppermute | solution.py:107
  114.2 66.1 %collective-permute-start.9 = (bf16[384,3200]{1,0:T(8,128)(2,1)}, bf16[384,3200]{1,0:T(8,128)(2,1)}, u32[]{:S(2)}, u32[]{:S(2)}) collective-permute-start(bf16[384,3200]{1,0:T(8,128)(2,1)} %constant_dynamic-update-slice_fusion.5), channel_id=1, source_target_pairs={{0,1},{1,0},{2,3},{3,2},{4,5},{5,4},{6,7},{7,6},{8,9},{9,8},{10,11... | collective-permute-start | bytes 7372808 | tf_op jit(solution)/shard_map/ppermute | solution.py:107
  137.6 35.9 %collective-permute-start.23 = (bf16[192,2048]{1,0:T(8,128)(2,1)}, bf16[192,2048]{1,0:T(8,128)(2,1)S(1)}, u32[]{:S(2)}, u32[]{:S(2)}) collective-permute-start(bf16[192,2048]{1,0:T(8,128)(2,1)} %get-tuple-element.35), channel_id=1, source_target_pairs={{0,16},{1,17},{2,18},{3,19},{4,20},{5,21},{6,22},{7,23},{8,24},{9,... | collective-permute-start | bytes 2359304 | tf_op jit(solution)/shard_map/ppermute | solution.py:107
  142.5 103.9 %collective-permute-start.24 = (bf16[192,2048]{1,0:T(8,128)(2,1)}, bf16[192,2048]{1,0:T(8,128)(2,1)}, u32[]{:S(2)}, u32[]{:S(2)}) collective-permute-start(bf16[192,2048]{1,0:T(8,128)(2,1)} %get-tuple-element.35), channel_id=1, source_target_pairs={{0,8},{1,9},{2,10},{3,11},{4,12},{5,13},{6,14},{7,15},{8,0},{9,1},... | collective-permute-start | bytes 2359304 | tf_op jit(solution)/shard_map/ppermute | solution.py:107
  149.9 26.1 %collective-permute-start.17 = (bf16[96,1536]{1,0:T(8,128)(2,1)S(1)}, bf16[96,1536]{1,0:T(8,128)(2,1)S(1)}, u32[]{:S(2)}, u32[]{:S(2)}) collective-permute-start(bf16[96,1536]{1,0:T(8,128)(2,1)S(1)} %collective-permute-done.13), channel_id=1, source_target_pairs={{0,2},{1,3},{2,0},{3,1},{4,6},{5,7},{6,4},{7,5},{8,10},{9,11},{10,... | collective-permute-start | bytes 884744 | tf_op jit(solution)/shard_map/ppermute | solution.py:107
  173.5 74.5 %collective-permute-start.26 = (bf16[192,2048]{1,0:T(8,128)(2,1)}, bf16[192,2048]{1,0:T(8,128)(2,1)}, u32[]{:S(2)}, u32[]{:S(2)}) collective-permute-start(bf16[192,2048]{1,0:T(8,128)(2,1)} %get-tuple-element.35), channel_id=1, source_target_pairs={{0,4},{1,5},{2,6},{3,7},{4,0},{5,1},{6,2},{7,3},{8,12},{9,13},{10,... | collective-permute-start | bytes 2359304 | tf_op jit(solution)/shard_map/ppermute | solution.py:107
  176.0 100.4 %collective-permute-start.39 = (bf16[384,1536]{1,0:T(8,128)(2,1)}, bf16[384,1536]{1,0:T(8,128)(2,1)}, u32[]{:S(2)}, u32[]{:S(2)}) collective-permute-start(bf16[384,1536]{1,0:T(8,128)(2,1)} %fusion.57), channel_id=1, source_target_pairs={{0,2},{1,3},{2,0},{3,1},{4,6},{5,7},{6,4},{7,5},{8,10},{9,11},{10,... | collective-permute-start | bytes 3538952 | tf_op jit(solution)/shard_map/ppermute | solution.py:107
  179.3 58.2 %collective-permute-start.18 = (bf16[384,1536]{1,0:T(8,128)(2,1)}, bf16[384,1536]{1,0:T(8,128)(2,1)}, u32[]{:S(2)}, u32[]{:S(2)}) collective-permute-start(bf16[384,1536]{1,0:T(8,128)(2,1)} %constant_dynamic-update-slice_fusion.11), channel_id=1, source_target_pairs={{0,1},{1,0},{2,3},{3,2},{4,5},{5,4},{6,7},{7,6},{8,9},{9,8},{10,11... | collective-permute-start | bytes 3538952 | tf_op jit(solution)/shard_map/ppermute | solution.py:107
  180.4 59.7 %collective-permute-start.19 = (bf16[384,1536]{1,0:T(8,128)(2,1)}, bf16[384,1536]{1,0:T(8,128)(2,1)}, u32[]{:S(2)}, u32[]{:S(2)}) collective-permute-start(bf16[384,1536]{1,0:T(8,128)(2,1)} %constant_dynamic-update-slice_fusion.16), channel_id=1, source_target_pairs={{0,1},{1,0},{2,3},{3,2},{4,5},{5,4},{6,7},{7,6},{8,9},{9,8},{10,11... | collective-permute-start | bytes 3538952 | tf_op jit(solution)/shard_map/ppermute | solution.py:107
  240.1 36.3 %collective-permute-start.25 = (bf16[192,2048]{1,0:T(8,128)(2,1)S(1)}, bf16[192,2048]{1,0:T(8,128)(2,1)S(1)}, u32[]{:S(2)}, u32[]{:S(2)}) collective-permute-start(bf16[192,2048]{1,0:T(8,128)(2,1)S(1)} %copy-done.51), channel_id=1, source_target_pairs={{0,8},{1,9},{2,10},{3,11},{4,12},{5,13},{6,14},{7,15},{8,0},{9,1},... | collective-permute-start | bytes 2359304 | tf_op jit(solution)/shard_map/ppermute | solution.py:107
  246.5 30.5 %collective-permute-start.27 = (bf16[192,2048]{1,0:T(8,128)(2,1)S(1)}, bf16[192,2048]{1,0:T(8,128)(2,1)S(1)}, u32[]{:S(2)}, u32[]{:S(2)}) collective-permute-start(bf16[192,2048]{1,0:T(8,128)(2,1)S(1)} %copy-done.51), channel_id=1, source_target_pairs={{0,4},{1,5},{2,6},{3,7},{4,0},{5,1},{6,2},{7,3},{8,12},{9,13},{10,... | collective-permute-start | bytes 2359304 | tf_op jit(solution)/shard_map/ppermute | solution.py:107
  248.1 26.1 %collective-permute-start.36 = (bf16[192,1024]{1,0:T(8,128)(2,1)S(1)}, bf16[192,1024]{1,0:T(8,128)(2,1)S(1)}, u32[]{:S(2)}, u32[]{:S(2)}) collective-permute-start(bf16[192,1024]{1,0:T(8,128)(2,1)S(1)} %copy-done.62), channel_id=1, source_target_pairs={{0,4},{1,5},{2,6},{3,7},{4,0},{5,1},{6,2},{7,3},{8,12},{9,13},{10,... | collective-permute-start | bytes 1179656 | tf_op jit(solution)/shard_map/ppermute | solution.py:107
  250.9 44.0 %collective-permute-start.20 = (bf16[384,1536]{1,0:T(8,128)(2,1)S(1)}, bf16[384,1536]{1,0:T(8,128)(2,1)S(1)}, u32[]{:S(2)}, u32[]{:S(2)}) collective-permute-start(bf16[384,1536]{1,0:T(8,128)(2,1)S(1)} %fusion.47), channel_id=1, source_target_pairs={{0,2},{1,3},{2,0},{3,1},{4,6},{5,7},{6,4},{7,5},{8,10},{9,11},{10,... | collective-permute-start | bytes 3538952 | tf_op jit(solution)/shard_map/ppermute | solution.py:107
  274.2 20.7 %collective-permute-start.28 = (bf16[192,2048]{1,0:T(8,128)(2,1)}, bf16[192,2048]{1,0:T(8,128)(2,1)S(1)}, u32[]{:S(2)}, u32[]{:S(2)}) collective-permute-start(bf16[192,2048]{1,0:T(8,128)(2,1)} %collective-permute-done.24), channel_id=1, source_target_pairs={{0,4},{1,5},{2,6},{3,7},{4,0},{5,1},{6,2},{7,3},{8,12},{9,13},{10,... | collective-permute-start | bytes 2359304 | tf_op jit(solution)/shard_map/ppermute | solution.py:107
  276.4 34.0 %collective-permute-start.40 = (bf16[384,1536]{1,0:T(8,128)(2,1)}, bf16[384,1536]{1,0:T(8,128)(2,1)S(1)}, u32[]{:S(2)}, u32[]{:S(2)}) collective-permute-start(bf16[384,1536]{1,0:T(8,128)(2,1)} %fusion.57), channel_id=1, source_target_pairs={{0,1},{1,0},{2,3},{3,2},{4,5},{5,4},{6,7},{7,6},{8,9},{9,8},{10,11... | collective-permute-start | bytes 3538952 | tf_op jit(solution)/shard_map/ppermute | solution.py:107
  276.5 34.0 %collective-permute-start.41 = (bf16[384,1536]{1,0:T(8,128)(2,1)}, bf16[384,1536]{1,0:T(8,128)(2,1)S(1)}, u32[]{:S(2)}, u32[]{:S(2)}) collective-permute-start(bf16[384,1536]{1,0:T(8,128)(2,1)} %collective-permute-done.39), channel_id=1, source_target_pairs={{0,1},{1,0},{2,3},{3,2},{4,5},{5,4},{6,7},{7,6},{8,9},{9,8},{10,11... | collective-permute-start | bytes 3538952 | tf_op jit(solution)/shard_map/ppermute | solution.py:107
  277.0 32.6 %collective-permute-start.29 = (bf16[192,2048]{1,0:T(8,128)(2,1)S(1)}, bf16[192,2048]{1,0:T(8,128)(2,1)S(1)}, u32[]{:S(2)}, u32[]{:S(2)}) collective-permute-start(bf16[192,2048]{1,0:T(8,128)(2,1)S(1)} %collective-permute-done.25), channel_id=1, source_target_pairs={{0,4},{1,5},{2,6},{3,7},{4,0},{5,1},{6,2},{7,3},{8,12},{9,13},{10,... | collective-permute-start | bytes 2359304 | tf_op jit(solution)/shard_map/ppermute | solution.py:107
  294.8 18.4 %collective-permute-start.21 = (bf16[384,1536]{1,0:T(8,128)(2,1)S(1)}, bf16[384,1536]{1,0:T(8,128)(2,1)S(1)}, u32[]{:S(2)}, u32[]{:S(2)}) collective-permute-start(bf16[384,1536]{1,0:T(8,128)(2,1)S(1)} %fusion.47), channel_id=1, source_target_pairs={{0,1},{1,0},{2,3},{3,2},{4,5},{5,4},{6,7},{7,6},{8,9},{9,8},{10,11... | collective-permute-start | bytes 3538952 | tf_op jit(solution)/shard_map/ppermute | solution.py:107
  294.9 18.4 %collective-permute-start.22 = (bf16[384,1536]{1,0:T(8,128)(2,1)S(1)}, bf16[384,1536]{1,0:T(8,128)(2,1)S(1)}, u32[]{:S(2)}, u32[]{:S(2)}) collective-permute-start(bf16[384,1536]{1,0:T(8,128)(2,1)S(1)} %collective-permute-done.20), channel_id=1, source_target_pairs={{0,1},{1,0},{2,3},{3,2},{4,5},{5,4},{6,7},{7,6},{8,9},{9,8},{10,11... | collective-permute-start | bytes 3538952 | tf_op jit(solution)/shard_map/ppermute | solution.py:107
  353.9 37.6 %collective-permute-start.62 = (bf16[768,1024]{1,0:T(8,128)(2,1)}, bf16[768,1024]{1,0:T(8,128)(2,1)}, u32[]{:S(2)}, u32[]{:S(2)}) collective-permute-start(bf16[768,1024]{1,0:T(8,128)(2,1)} %fusion.92), channel_id=1, source_target_pairs={{0,4},{1,5},{2,6},{3,7},{4,0},{5,1},{6,2},{7,3},{8,12},{9,13},{10,... | collective-permute-start | bytes 4718600 | tf_op jit(solution)/shard_map/ppermute | solution.py:107
  359.6 65.7 %collective-permute-start.59 = (bf16[768,1024]{1,0:T(8,128)(2,1)}, bf16[768,1024]{1,0:T(8,128)(2,1)}, u32[]{:S(2)}, u32[]{:S(2)}) collective-permute-start(bf16[768,1024]{1,0:T(8,128)(2,1)} %fusion.89), channel_id=1, source_target_pairs={{0,4},{1,5},{2,6},{3,7},{4,0},{5,1},{6,2},{7,3},{8,12},{9,13},{10,... | collective-permute-start | bytes 4718600 | tf_op jit(solution)/shard_map/ppermute | solution.py:107
  380.0 75.8 %collective-permute-start.56 = (bf16[768,1024]{1,0:T(8,128)(2,1)}, bf16[768,1024]{1,0:T(8,128)(2,1)S(1)}, u32[]{:S(2)}, u32[]{:S(2)}) collective-permute-start(bf16[768,1024]{1,0:T(8,128)(2,1)} %fusion.86), channel_id=1, source_target_pairs={{0,4},{1,5},{2,6},{3,7},{4,0},{5,1},{6,2},{7,3},{8,12},{9,13},{10,... | collective-permute-start | bytes 4718600 | tf_op jit(solution)/shard_map/ppermute | solution.py:107
  388.1 100.2 %collective-permute-start.42 = (bf16[768,1536]{1,0:T(8,128)(2,1)S(1)}, bf16[768,1536]{1,0:T(8,128)(2,1)}, u32[]{:S(2)}, u32[]{:S(2)}) collective-permute-start(bf16[768,1536]{1,0:T(8,128)(2,1)S(1)} %slice.327), channel_id=1, source_target_pairs={{0,1},{1,0},{2,3},{3,2},{4,5},{5,4},{6,7},{7,6},{8,9},{9,8},{10,11... | collective-permute-start | bytes 7077896 | tf_op jit(solution)/shard_map/ppermute | solution.py:107
  388.4 104.6 %collective-permute-start.37 = (bf16[768,1536]{1,0:T(8,128)(2,1)S(1)}, bf16[768,1536]{1,0:T(8,128)(2,1)}, u32[]{:S(2)}, u32[]{:S(2)}) collective-permute-start(bf16[768,1536]{1,0:T(8,128)(2,1)S(1)} %slice.323), channel_id=1, source_target_pairs={{0,1},{1,0},{2,3},{3,2},{4,5},{5,4},{6,7},{7,6},{8,9},{9,8},{10,11... | collective-permute-start | bytes 7077896 | tf_op jit(solution)/shard_map/ppermute | solution.py:107
  395.9 64.5 %collective-permute-start.63 = (bf16[384,1024]{1,0:T(8,128)(2,1)S(1)}, bf16[384,1024]{1,0:T(8,128)(2,1)S(1)}, u32[]{:S(2)}, u32[]{:S(2)}) collective-permute-start(bf16[384,1024]{1,0:T(8,128)(2,1)S(1)} %slice.497), channel_id=1, source_target_pairs={{0,8},{1,9},{2,10},{3,11},{4,12},{5,13},{6,14},{7,15},{8,0},{9,1},... | collective-permute-start | bytes 2359304 | tf_op jit(solution)/shard_map/ppermute | solution.py:107
  429.6 32.3 %collective-permute-start.60 = (bf16[384,1024]{1,0:T(8,128)(2,1)S(1)}, bf16[384,1024]{1,0:T(8,128)(2,1)S(1)}, u32[]{:S(2)}, u32[]{:S(2)}) collective-permute-start(bf16[384,1024]{1,0:T(8,128)(2,1)S(1)} %slice.498), channel_id=1, source_target_pairs={{0,8},{1,9},{2,10},{3,11},{4,12},{5,13},{6,14},{7,15},{8,0},{9,1},... | collective-permute-start | bytes 2359304 | tf_op jit(solution)/shard_map/ppermute | solution.py:107
  458.7 29.1 %collective-permute-start.57 = (bf16[384,1024]{1,0:T(8,128)(2,1)S(1)}, bf16[384,1024]{1,0:T(8,128)(2,1)S(1)}, u32[]{:S(2)}, u32[]{:S(2)}) collective-permute-start(bf16[384,1024]{1,0:T(8,128)(2,1)S(1)} %slice.499), channel_id=1, source_target_pairs={{0,8},{1,9},{2,10},{3,11},{4,12},{5,13},{6,14},{7,15},{8,0},{9,1},... | collective-permute-start | bytes 2359304 | tf_op jit(solution)/shard_map/ppermute | solution.py:107
  461.5 83.2 %collective-permute-start.64 = (bf16[192,1024]{1,0:T(8,128)(2,1)}, bf16[192,1024]{1,0:T(8,128)(2,1)}, u32[]{:S(2)}, u32[]{:S(2)}) collective-permute-start(bf16[192,1024]{1,0:T(8,128)(2,1)} %slice.503), channel_id=1, source_target_pairs={{0,16},{1,17},{2,18},{3,19},{4,20},{5,21},{6,22},{7,23},{8,24},{9,... | collective-permute-start | bytes 1179656 | tf_op jit(solution)/shard_map/ppermute | solution.py:107
  462.3 45.7 %collective-permute-start.61 = (bf16[192,1024]{1,0:T(8,128)(2,1)S(1)}, bf16[192,1024]{1,0:T(8,128)(2,1)S(1)}, u32[]{:S(2)}, u32[]{:S(2)}) collective-permute-start(bf16[192,1024]{1,0:T(8,128)(2,1)S(1)} %slice.504), channel_id=1, source_target_pairs={{0,16},{1,17},{2,18},{3,19},{4,20},{5,21},{6,22},{7,23},{8,24},{9,... | collective-permute-start | bytes 1179656 | tf_op jit(solution)/shard_map/ppermute | solution.py:107
  488.0 24.2 %collective-permute-start.58 = (bf16[192,1024]{1,0:T(8,128)(2,1)S(1)}, bf16[192,1024]{1,0:T(8,128)(2,1)S(1)}, u32[]{:S(2)}, u32[]{:S(2)}) collective-permute-start(bf16[192,1024]{1,0:T(8,128)(2,1)S(1)} %slice.505), channel_id=1, source_target_pairs={{0,16},{1,17},{2,18},{3,19},{4,20},{5,21},{6,22},{7,23},{8,24},{9,... | collective-permute-start | bytes 1179656 | tf_op jit(solution)/shard_map/ppermute | solution.py:107
  490.8 56.1 %collective-permute-start.43 = (bf16[384,1536]{1,0:T(8,128)(2,1)S(1)}, bf16[384,1536]{1,0:T(8,128)(2,1)}, u32[]{:S(2)}, u32[]{:S(2)}) collective-permute-start(bf16[384,1536]{1,0:T(8,128)(2,1)S(1)} %slice.495), channel_id=1, source_target_pairs={{0,2},{1,3},{2,0},{3,1},{4,6},{5,7},{6,4},{7,5},{8,10},{9,11},{10,... | collective-permute-start | bytes 3538952 | tf_op jit(solution)/shard_map/ppermute | solution.py:107
  496.5 271.7 %collective-permute-start.38 = (bf16[384,1536]{1,0:T(8,128)(2,1)}, bf16[384,1536]{1,0:T(8,128)(2,1)}, u32[]{:S(2)}, u32[]{:S(2)}) collective-permute-start(bf16[384,1536]{1,0:T(8,128)(2,1)} %slice.496), channel_id=1, source_target_pairs={{0,2},{1,3},{2,0},{3,1},{4,6},{5,7},{6,4},{7,5},{8,10},{9,11},{10,... | collective-permute-start | bytes 3538952 | tf_op jit(solution)/shard_map/ppermute | solution.py:107
  625.0 25.9 %collective-permute-start.50 = (bf16[384,1536]{1,0:T(8,128)(2,1)S(1)}, bf16[384,1536]{1,0:T(8,128)(2,1)S(1)}, u32[]{:S(2)}, u32[]{:S(2)}) collective-permute-start(bf16[384,1536]{1,0:T(8,128)(2,1)S(1)} %copy-done.47), channel_id=1, source_target_pairs={{0,1},{1,0},{2,3},{3,2},{4,5},{5,4},{6,7},{7,6},{8,9},{9,8},{10,11... | collective-permute-start | bytes 3538952 | tf_op jit(solution)/shard_map/ppermute | solution.py:107
  625.2 17.5 %collective-permute-start.51 = (bf16[384,1536]{1,0:T(8,128)(2,1)S(1)}, bf16[384,1536]{1,0:T(8,128)(2,1)S(1)}, u32[]{:S(2)}, u32[]{:S(2)}) collective-permute-start(bf16[384,1536]{1,0:T(8,128)(2,1)S(1)} %convolution_convert_fusion.4), channel_id=1, source_target_pairs={{0,1},{1,0},{2,3},{3,2},{4,5},{5,4},{6,7},{7,6},{8,9},{9,8},{10,11... | collective-permute-start | bytes 3538952 | tf_op jit(solution)/shard_map/ppermute | solution.py:107
  626.9 95.7 %collective-permute-start.44 = (bf16[384,3072]{1,0:T(8,128)(2,1)S(1)}, bf16[384,3072]{1,0:T(8,128)(2,1)S(1)}, u32[]{:S(2)}, u32[]{:S(2)}) collective-permute-start(bf16[384,3072]{1,0:T(8,128)(2,1)S(1)} %convolution_convert_fusion.3), channel_id=1, source_target_pairs={{0,1},{1,0},{2,3},{3,2},{4,5},{5,4},{6,7},{7,6},{8,9},{9,8},{10,11... | collective-permute-start | bytes 7077896 | tf_op jit(solution)/shard_map/ppermute | solution.py:107
  641.7 80.9 %collective-permute-start.46 = (bf16[384,3072]{1,0:T(8,128)(2,1)S(1)}, bf16[384,3072]{1,0:T(8,128)(2,1)S(1)}, u32[]{:S(2)}, u32[]{:S(2)}) collective-permute-start(bf16[384,3072]{1,0:T(8,128)(2,1)S(1)} %add_convert_fusion), channel_id=1, source_target_pairs={{0,2},{1,3},{2,0},{3,1},{4,6},{5,7},{6,4},{7,5},{8,10},{9,11},{10,... | collective-permute-start | bytes 7077896 | tf_op jit(solution)/shard_map/ppermute | solution.py:107
  643.5 77.0 %collective-permute-start.52 = (bf16[384,1536]{1,0:T(8,128)(2,1)S(1)}, bf16[384,1536]{1,0:T(8,128)(2,1)S(1)}, u32[]{:S(2)}, u32[]{:S(2)}) collective-permute-start(bf16[384,1536]{1,0:T(8,128)(2,1)S(1)} %add_convert_fusion.3), channel_id=1, source_target_pairs={{0,2},{1,3},{2,0},{3,1},{4,6},{5,7},{6,4},{7,5},{8,10},{9,11},{10,... | collective-permute-start | bytes 3538952 | tf_op jit(solution)/shard_map/ppermute | solution.py:107
  723.9 43.5 %collective-permute-start.47 = (bf16[192,3072]{1,0:T(8,128)(2,1)S(1)}, bf16[192,3072]{1,0:T(8,128)(2,1)S(1)}, u32[]{:S(2)}, u32[]{:S(2)}) collective-permute-start(bf16[192,3072]{1,0:T(8,128)(2,1)S(1)} %slice.494), channel_id=1, source_target_pairs={{0,8},{1,9},{2,10},{3,11},{4,12},{5,13},{6,14},{7,15},{8,0},{9,1},... | collective-permute-start | bytes 3538952 | tf_op jit(solution)/shard_map/ppermute | solution.py:107
  737.5 35.3 %collective-permute-start.54 = (bf16[96,1536]{1,0:T(8,128)(2,1)S(1)}, bf16[96,1536]{1,0:T(8,128)(2,1)S(1)}, u32[]{:S(2)}, u32[]{:S(2)}) collective-permute-start(bf16[96,1536]{1,0:T(8,128)(2,1)S(1)} %slice.506), channel_id=1, source_target_pairs={{0,16},{1,17},{2,18},{3,19},{4,20},{5,21},{6,22},{7,23},{8,24},{9,... | collective-permute-start | bytes 884744 | tf_op jit(solution)/shard_map/ppermute | solution.py:107
  767.7 27.4 %collective-permute-start.48 = (bf16[96,3072]{1,0:T(8,128)(2,1)S(1)}, bf16[96,3072]{1,0:T(8,128)(2,1)S(1)}, u32[]{:S(2)}, u32[]{:S(2)}) collective-permute-start(bf16[96,3072]{1,0:T(8,128)(2,1)S(1)} %slice.501), channel_id=1, source_target_pairs={{0,16},{1,17},{2,18},{3,19},{4,20},{5,21},{6,22},{7,23},{8,24},{9,... | collective-permute-start | bytes 1769480 | tf_op jit(solution)/shard_map/ppermute | solution.py:107
  773.0 24.0 %collective-permute-start.55 = (bf16[48,1536]{1,0:T(8,128)(2,1)S(1)}, bf16[48,1536]{1,0:T(8,128)(2,1)S(1)}, u32[]{:S(2)}, u32[]{:S(2)}) collective-permute-start(bf16[48,1536]{1,0:T(8,128)(2,1)S(1)} %slice.508), channel_id=1, source_target_pairs={{0,4},{1,5},{2,6},{3,7},{4,0},{5,1},{6,2},{7,3},{8,12},{9,13},{10,... | collective-permute-start | bytes 442376 | tf_op jit(solution)/shard_map/ppermute | solution.py:107
  (103 other events, 1858.0 us)
